TPU v7x, 32 devices: a whole 2x2x4 slice. The times are simulated.
32 devices in a mesh: dp: 8 (over y, x, core), mp: 4 (over z).
Axes of the slice: x: 2, y: 2, z: 4, core: 2. Of those that a mesh axis runs over, the one named last changes fastest.
Arguments:
- tokens: bfloat16 [16384, 2048], P(('dp', 'mp')), may hold values from -6 to 6
- lengths: int32 [8], P('dp'), may hold values from 128 to 2048, as said below
- cotangent: bfloat16 [16384, 2048], P(('dp', 'mp')), may hold values from -6 to 6
- first_gain: float32 [2048], replicated, may hold values from 0.25 to 1.75
- first_shift: float32 [2048], replicated, may hold values from -4 to 4
- second_gain: float32 [2048], replicated, may hold values from 0.25 to 1.75
- second_shift: float32 [2048], replicated, may hold values from -4 to 4
- attend_weight: bfloat16 [3, 2048, 2048], P(None, None, 'mp'), may hold values from -0.125 to 0.125
- attend_bias: float32 [3, 2048], P(None, 'mp'), may hold values from -6 to 6
- merge_weight: bfloat16 [2048, 2048], P('mp'), may hold values from -0.5 to 0.5
- merge_bias: float32 [2048], replicated, may hold values from -4 to 4
- expand_weight: bfloat16 [2048, 8192], P(None, 'mp'), may hold values from -0.125 to 0.125
- expand_bias: float32 [8192], P('mp'), may hold values from -6 to 6
- contract_weight: bfloat16 [8192, 2048], P('mp'), may hold values from -0.0625 to 0.0625
- contract_bias: float32 [2048], replicated, may hold values from -4 to 4
Outputs:
- layer_output: bfloat16 [16384, 2048], P(('dp', 'mp'))
- tokens_grad: bfloat16 [16384, 2048], P(('dp', 'mp'))
- first_gain_grad: float32 [2048], replicated
- first_shift_grad: float32 [2048], replicated
- second_gain_grad: float32 [2048], replicated
- second_shift_grad: float32 [2048], replicated
- attend_weight_grad: float32 [3, 2048, 2048], P(None, None, 'mp')
- attend_bias_grad: float32 [3, 2048], P(None, 'mp')
- merge_weight_grad: float32 [2048, 2048], P('mp')
- merge_bias_grad: float32 [2048], replicated
- expand_weight_grad: float32 [2048, 8192], P(None, 'mp')
- expand_bias_grad: float32 [8192], P('mp')
- contract_weight_grad: float32 [8192, 2048], P('mp')
- contract_bias_grad: float32 [2048], replicated
Inputs may be any that keep to these rules, and one draw needn't show every extreme that they name: Sequence b holds lengths[b] real tokens followed by padding; some sequence has 2048.
All inputs are finite; a program needn't handle non-finite values.
Results may differ from a plain program's by a relative error of at most 0.011.
Values may be sent and summed in bfloat16 or wider, within the bound.
No kernel may reach another device: no remote copies, remote signals or barrier semaphores. Data moves between devices by JAX's collectives and lax.ppermute only.
A program may use at most 320 MiB of HBM per device.

v0:
```python
from functools import partial

import jax
import jax.numpy as jnp
from jax import lax
from jax.sharding import PartitionSpec as P

HD = 256
ROT = 64


norm_eps = 1e-05
masked_score = -1e30


def layer_norm(inputs, gain_values, shift_values):
    average = jnp.mean(inputs, axis=-1, keepdims=True)
    centred = inputs - average
    variance = jnp.mean(centred * centred, axis=-1, keepdims=True)
    return centred * lax.rsqrt(variance + norm_eps) * gain_values + shift_values


def standardize(inputs):
    average = jnp.mean(inputs, axis=-1, keepdims=True)
    centred = inputs - average
    variance = jnp.mean(centred * centred, axis=-1, keepdims=True)
    inverse = lax.rsqrt(variance + norm_eps)
    return (centred * inverse, inverse)


def rotary_tables(length, rotated):
    halfway = rotated // 2
    channel = jnp.arange(halfway).astype(jnp.float32)
    frequency = 1.0 / 10000.0 ** (channel * 2.0 / rotated)
    positions = jnp.arange(length).astype(jnp.float32)
    angles = positions[:, None] * frequency[None, :]
    angles = jnp.concatenate([angles, angles], axis=1)
    return (jnp.cos(angles), jnp.sin(angles))


def rotate(per_head, cosine, sine_table, rotated):
    halfway = rotated // 2
    leading = per_head[..., :rotated]
    turned = jnp.concatenate([-leading[..., halfway:], leading[..., :halfway]], axis=-1)
    rotated_part = leading * cosine[:, None, :] + turned * sine_table[:, None, :]
    return jnp.concatenate([rotated_part, per_head[..., rotated:]], axis=-1)


def unrotate(grads_in, cosine, sine_table, rotated):
    halfway = rotated // 2
    leading = grads_in[..., :rotated]
    turned = leading * sine_table[:, None, :]
    back_part = leading * cosine[:, None, :] + jnp.concatenate(
        [turned[..., halfway:], -turned[..., :halfway]], axis=-1
    )
    return jnp.concatenate([back_part, grads_in[..., rotated:]], axis=-1)


def block_mask(block_index, block_rows, seq_span, seq_length):
    query_places = block_index * block_rows + jnp.arange(block_rows)
    key_places = jnp.arange(seq_span)
    return (key_places[None, :] <= query_places[:, None]) & (key_places[None, :] < seq_length)


def attend_sequence(queries, keys_all, values_all, seq_length):
    seq_span, head_count, head_size = queries.shape
    block_rows = min(512, seq_span)
    block_count = seq_span // block_rows

    def one_block(block_item):
        query_block, block_index = block_item
        allowed = block_mask(block_index, block_rows, seq_span, seq_length)
        scores = jnp.einsum(
            "qhd,khd->hqk", query_block, keys_all, preferred_element_type=jnp.float32
        )
        scores = jnp.where(allowed[None], scores, masked_score)
        highest = jnp.max(scores, axis=-1, keepdims=True)
        exponent = jnp.exp(scores - highest)
        row_total = jnp.sum(exponent, axis=-1, keepdims=True)
        weights_low = (exponent / row_total).astype(jnp.bfloat16)
        outputs = jnp.einsum(
            "hqk,khd->qhd", weights_low, values_all, preferred_element_type=jnp.float32
        )
        return (outputs, (highest + jnp.log(row_total))[..., 0])

    blocked = queries.reshape(block_count, block_rows, head_count, head_size)
    outputs, log_sums = lax.map(one_block, (blocked, jnp.arange(block_count)))
    return (outputs.reshape(seq_span, head_count, head_size), log_sums)


def attend_backward(queries, keys_all, values_all, seq_length, log_sums, grad_mixed):
    seq_span, head_count, head_size = queries.shape
    block_rows = min(512, seq_span)
    block_count = seq_span // block_rows

    def one_block(carried, block_item):
        grad_keys, grad_values = carried
        query_block, block_index, log_block, grad_block = block_item
        allowed = block_mask(block_index, block_rows, seq_span, seq_length)
        scores = jnp.einsum(
            "qhd,khd->hqk", query_block, keys_all, preferred_element_type=jnp.float32
        )
        scores = jnp.where(allowed[None], scores, masked_score)
        weights = jnp.exp(scores - log_block[..., None])
        grad_weights = jnp.einsum(
            "qhd,khd->hqk", grad_block, values_all, preferred_element_type=jnp.float32
        )
        centre_term = jnp.sum(grad_weights * weights, axis=-1, keepdims=True)
        grad_scores = (weights * (grad_weights - centre_term)).astype(jnp.bfloat16)
        grad_queries = jnp.einsum(
            "hqk,khd->qhd", grad_scores, keys_all, preferred_element_type=jnp.float32
        )
        grad_keys = grad_keys + jnp.einsum(
            "hqk,qhd->khd", grad_scores, query_block, preferred_element_type=jnp.float32
        )
        grad_values = grad_values + jnp.einsum(
            "hqk,qhd->khd",
            weights.astype(jnp.bfloat16),
            grad_block,
            preferred_element_type=jnp.float32,
        )
        return ((grad_keys, grad_values), grad_queries)

    blocked = queries.reshape(block_count, block_rows, head_count, head_size)
    grad_blocked = grad_mixed.reshape(block_count, block_rows, head_count, head_size)
    empty_grads = jnp.zeros((seq_span, head_count, head_size), jnp.float32)
    (grad_keys, grad_values), grad_queries = lax.scan(
        one_block,
        (empty_grads, empty_grads),
        (blocked, jnp.arange(block_count), log_sums, grad_blocked),
    )
    return (grad_queries.reshape(seq_span, head_count, head_size), grad_keys, grad_values)


def on_device(
    tokens,
    lengths,
    cotangent,
    first_gain,
    first_shift,
    second_gain,
    second_shift,
    attend_weight,
    attend_bias,
    merge_weight,
    merge_bias,
    expand_weight,
    expand_bias,
    contract_weight,
    contract_bias,
):
    rows_here = tokens.shape[0]
    seq_count = lengths.shape[0]
    group_rows = rows_here * lax.axis_size("mp")
    seq_span = group_rows // seq_count
    local_width = attend_weight.shape[2]
    local_heads = local_width // HD
    head_scale = HD ** (-0.5)
    row_ids = lax.axis_index("mp") * rows_here + jnp.arange(rows_here)
    owner_table = (row_ids // seq_span)[:, None] == jnp.arange(seq_count)[None, :]
    row_lengths = jnp.sum(jnp.where(owner_table, lengths[None, :], 0), axis=1)
    valid_rows = row_ids % seq_span < row_lengths
    inputs = tokens.astype(jnp.float32)
    normed_one = layer_norm(inputs, first_gain, first_shift).astype(jnp.bfloat16)
    normed_two = layer_norm(inputs, second_gain, second_shift).astype(jnp.bfloat16)
    full_one, full_two = (
        lax.all_gather(normed_one, "mp", axis=0, tiled=True),
        lax.all_gather(normed_two, "mp", axis=0, tiled=True),
    )
    projected = jnp.einsum(
        "td,cde->cte", full_one, attend_weight, preferred_element_type=jnp.float32
    )
    projected = projected + attend_bias[:, None, :]
    per_head = projected.reshape(3, seq_count, seq_span, local_heads, HD)
    cosine, sine_table = rotary_tables(seq_span, ROT)
    queries = (rotate(per_head[0], cosine, sine_table, ROT) * head_scale).astype(jnp.bfloat16)
    keys_all = rotate(per_head[1], cosine, sine_table, ROT).astype(jnp.bfloat16)
    values_all = per_head[2].astype(jnp.bfloat16)
    attended, log_sums = lax.map(
        lambda seq_item: attend_sequence(*seq_item), (queries, keys_all, values_all, lengths)
    )
    mixed = attended.reshape(group_rows, local_width).astype(jnp.bfloat16)
    hidden_pre = jnp.dot(full_two, expand_weight, preferred_element_type=jnp.float32) + expand_bias
    activated = jax.nn.gelu(hidden_pre, approximate=False).astype(jnp.bfloat16)
    attn_share = lax.psum_scatter(
        jnp.dot(mixed, merge_weight, preferred_element_type=jnp.float32),
        "mp",
        scatter_dimension=0,
        tiled=True,
    )
    feed_share = lax.psum_scatter(
        jnp.dot(activated, contract_weight, preferred_element_type=jnp.float32).astype(
            jnp.bfloat16
        ),
        "mp",
        scatter_dimension=0,
        tiled=True,
    ).astype(jnp.float32)
    branch_share = attn_share + feed_share
    layer_output = (inputs + branch_share + merge_bias + contract_bias).astype(jnp.bfloat16)
    grad_out = jnp.where(valid_rows[:, None], cotangent, jnp.zeros_like(cotangent))
    full_cot = lax.all_gather(grad_out, "mp", axis=0, tiled=True)
    bias_total = jnp.sum(full_cot, axis=0, dtype=jnp.float32)
    contract_weight_grad = jnp.einsum(
        "tf,td->fd", activated, full_cot, preferred_element_type=jnp.float32
    )
    grad_act = jnp.einsum(
        "td,fd->tf", full_cot, contract_weight, preferred_element_type=jnp.float32
    ).astype(jnp.bfloat16)
    gelu_value, gelu_pull = jax.vjp(partial(jax.nn.gelu, approximate=False), hidden_pre)
    grad_hidden = gelu_pull(grad_act.astype(jnp.float32))[0].astype(jnp.bfloat16)
    expand_weight_grad = jnp.einsum(
        "td,tf->df", full_two, grad_hidden, preferred_element_type=jnp.float32
    )
    expand_bias_grad = jnp.sum(grad_hidden, axis=0, dtype=jnp.float32)
    grad_two = jnp.einsum(
        "tf,df->td", grad_hidden, expand_weight, preferred_element_type=jnp.float32
    )
    merge_weight_grad = jnp.einsum("tf,td->fd", mixed, full_cot, preferred_element_type=jnp.float32)
    grad_mixed = jnp.einsum(
        "td,fd->tf", full_cot, merge_weight, preferred_element_type=jnp.float32
    ).astype(jnp.bfloat16)
    grad_heads = grad_mixed.reshape(seq_count, seq_span, local_heads, HD)
    grad_queries, grad_keys, grad_values = lax.map(
        lambda seq_item: attend_backward(*seq_item),
        (queries, keys_all, values_all, lengths, log_sums, grad_heads),
    )
    grad_projected = (
        jnp.stack(
            [
                unrotate(grad_queries, cosine, sine_table, ROT) * head_scale,
                unrotate(grad_keys, cosine, sine_table, ROT),
                grad_values,
            ]
        )
        .reshape(3, group_rows, local_width)
        .astype(jnp.bfloat16)
    )
    attend_weight_grad = jnp.einsum(
        "td,cte->cde", full_one, grad_projected, preferred_element_type=jnp.float32
    )
    attend_bias_grad = jnp.sum(grad_projected, axis=1, dtype=jnp.float32)
    grad_one = jnp.einsum(
        "cte,cde->td", grad_projected, attend_weight, preferred_element_type=jnp.float32
    )
    (
        attend_weight_grad,
        attend_bias_grad,
        merge_weight_grad,
        contract_weight_grad,
        expand_weight_grad,
        expand_bias_grad,
        bias_total,
    ) = lax.psum(
        (
            attend_weight_grad,
            attend_bias_grad,
            merge_weight_grad,
            contract_weight_grad,
            expand_weight_grad,
            expand_bias_grad,
            bias_total,
        ),
        "dp",
    )
    full_inputs = lax.all_gather(tokens, "mp", axis=0, tiled=True).astype(jnp.float32)
    full_hat, full_inverse = standardize(full_inputs)
    first_gain_grad = jnp.sum(grad_one * full_hat, axis=0)
    first_shift_grad = jnp.sum(grad_one, axis=0)
    second_gain_grad = jnp.sum(grad_two * full_hat, axis=0)
    second_shift_grad = jnp.sum(grad_two, axis=0)
    weighted = grad_one * first_gain + grad_two * second_gain
    weighted_rows = lax.psum_scatter(weighted, "mp", scatter_dimension=0, tiled=True)
    own_hat, own_inverse = standardize(inputs)
    input_term = (
        weighted_rows
        - jnp.mean(weighted_rows, axis=-1, keepdims=True)
        - own_hat * jnp.mean(weighted_rows * own_hat, axis=-1, keepdims=True)
    ) * own_inverse
    tokens_grad = (grad_out.astype(jnp.float32) + input_term).astype(jnp.bfloat16)
    first_gain_grad, first_shift_grad, second_gain_grad, second_shift_grad = lax.psum(
        (first_gain_grad, first_shift_grad, second_gain_grad, second_shift_grad), ("dp", "mp")
    )
    return (
        layer_output,
        tokens_grad,
        first_gain_grad,
        first_shift_grad,
        second_gain_grad,
        second_shift_grad,
        attend_weight_grad,
        attend_bias_grad,
        merge_weight_grad,
        bias_total,
        expand_weight_grad,
        expand_bias_grad,
        contract_weight_grad,
        bias_total,
    )


def solution(mesh):
    return jax.shard_map(
        on_device,
        mesh=mesh,
        in_specs=(
            P(("dp", "mp"), None),
            P("dp"),
            P(("dp", "mp"), None),
            P(),
            P(),
            P(),
            P(),
            P(None, None, "mp"),
            P(None, "mp"),
            P("mp", None),
            P(),
            P(None, "mp"),
            P("mp"),
            P("mp", None),
            P(),
        ),
        out_specs=(
            P(("dp", "mp"), None),
            P(("dp", "mp"), None),
            P(),
            P(),
            P(),
            P(),
            P(None, None, "mp"),
            P(None, "mp"),
            P("mp", None),
            P(),
            P(None, "mp"),
            P("mp"),
            P("mp", None),
            P(),
        ),
        check_vma=False,
    )
```

profile of v0, /device:TPU:0, one launch (start us, length us, event | category | flops | bytes accessed | tf_op | source)
XLA Modules:
  0.0 2108.9 jit_solution(10683665403976400073)
XLA Ops:
  26.6 141.1 %all-gather.5.cloned.1.call-done = bf16[2048,2048]{1,0:T(8,128)(2,1)} async-done(((bf16[512,2048]{1,0:T(8,128)(2,1)}), bf16[2048,2048]{1,0:T(8,128)(2,1)}) %all-gather.5.cloned.1.call-update) | async-done | bytes 8388624 | tf_op jit(solution)/shard_map/all_gather | solution.py:167
  167.7 18.0 add_bitcast_fusion
  203.9 113.2 %all-gather.9.cloned.1.call-done = bf16[2048,2048]{1,0:T(8,128)(2,1)} async-done(((bf16[512,2048]{1,0:T(8,128)(2,1)}), bf16[2048,2048]{1,0:T(8,128)(2,1)}) %all-gather.9.cloned.1.call-update) | async-done | bytes 8388624 | tf_op jit(solution)/shard_map/all_gather | solution.py:202
  317.1 9.2 convolution_convert_fusion.1
  390.5 49.1 %while.47 = (s32[]{:T(128)}, bf16[4,512,2,256]{3,1,2,0:T(8,128)(2,1)}, f32[4,2,512]{2,1,0:T(2,128)S(1)}, s32[4]{0:T(128)S(1)}, s32[]{:T(128)}, /*index=5*/bf16[4...) while((s32[]{:T(128)}, ...), condition=%wide.region_5.6_spmd, body=%wide.region_2.5_spmd.sunk | while | flops 2168456704 | bytes 60334316 | solution.py:87
  439.6 106.9 %while.48 = (s32[]{:T(128)}, f32[2048,2,256]{0,2,1:T(8,128)}, f32[2048,2,256]{0,2,1:T(8,128)}, f32[4,512,2,256]{3,1,0,2:T(8,128)}, bf16[4,512,2,256]{3,1,2,0:T(8...) while((s32[]{:T(128)}, f32[2048,2,256]{0,2,1:T(8,128)}, ...), condition=%wide.region_10.11_spmd.clone, body=%wide.region_8.10_spmd.clone.sunk | while | flops 5400167936 | bytes 111186184 | solution.py:127
  590.8 14.0 copy.84
  613.4 18.8 fusion.54
  632.3 59.3 %multiply_convert_fusion.1 = (bf16[2048,2048]{1,0:T(8,128)(2,1)}, f32[2048,2048]{1,0:T(8,128)}, f32[2048,2048]{1,0:T(8,128)}) fusion(f32[2048]{0:T(1024)S(1)} %copy-done.46, bf16[2048,2048]{1,0:T(8,128)(2,1)} %all-gather.7.cloned.1.call-done, bf16[2048,2048]{1,0:T(8,128)(2,1)} %param.30), kind=kOutput, calls=%fused_computation.70 | convolution fusion | flops 17456693248 | bytes 58728448 | tf_op jit(solution)/shard_map/dot_general | solution.py:183
  697.6 31.4 %convert_reduce_fusion.1 = (f32[2048]{0:T(1024)}, bf16[2048,2048]{1,0:T(8,128)(2,1)}) fusion(f32[2048,2048]{1,0:T(8,128)} %get-tuple-element.363, bf16[2048,2048]{1,0:T(8,128)(2,1)S(1)} %copy-done.16, bf16[2048,2048]{1,0:T(8,128)(2,1)} %param.32, f32[2048,2048]{1,0:T(8,128)} %get-tuple-element.393, f32[2048]{0:T(1024)S(1)} %copy-done.46), kind=kOutput, calls=%fused_computation.68 | convolution fusion | flops 17259558912 | bytes 58736640 | tf_op jit(solution)/shard_map/td,fd->tf/dot_general | solution.py:207
  729.0 24.5 %fusion.103 = f32[2048,2048]{1,0:T(8,128)} fusion(bf16[2048,2048]{1,0:T(8,128)(2,1)} %all-gather.7.cloned.1.call-done, bf16[2048,2048]{1,0:T(8,128)(2,1)} %get-tuple-element.395), kind=kOutput, calls=%fused_computation.174 | convolution fusion | flops 17179869184 | bytes 33554432 | tf_op jit(solution)/shard_map/td,tf->df/dot_general | solution.py:212
  753.6 21.3 %fusion.104 = f32[2048,2048]{1,0:T(8,128)} fusion(bf16[2048,2048]{1,0:T(8,128)(2,1)S(1)} %copy-done.47, bf16[2048,2048]{1,0:T(8,128)(2,1)S(1)} %copy-done.16), kind=kOutput, calls=%fused_computation.175 | convolution fusion | flops 17179869184 | bytes 33554432 | tf_op jit(solution)/shard_map/tf,td->fd/dot_general | solution.py:204
  785.0 19.2 fusion.92
  804.2 33.3 %fusion.93 = (f32[2048]{0:T(1024)S(1)}, f32[2048]{0:T(1024)S(1)}, f32[2048,2048]{1,0:T(8,128)}, f32[2048]{0:T(1024)S(1)}, f32[2048]{0:T(1024)S(1)}) fusion(f32[2048]{0:T(1024)S(1)} %add_rsqrt_fusion, f32[2048]{0:T(1024)S(1)} %broadcast_multiply_fusion.1, bf16[2048,2048]{1,0:T(8,128)(2,1)} %all-gather.11.cloned.1.call-done, f32[2048]{0:T(1024)S(1)} %copy-done.36, ...), kind=kOutput, calls=%fused_computation.165 | convolution fusion | flops 17230192640 | bytes 58785792 | tf_op jit(solution)/shard_map/tf,df->td/dot_general | solution.py:216
  837.5 24.5 %convolution_convert_fusion = bf16[2048,2048]{1,0:T(8,128)(2,1)} fusion(bf16[2048,2048]{1,0:T(8,128)(2,1)} %get-tuple-element.362, bf16[2048,2048]{1,0:T(8,128)(2,1)} %param.32), kind=kOutput, calls=%fused_computation.90 | convolution fusion | flops 17184063488 | bytes 25165824 | tf_op jit(solution)/shard_map/dot_general | solution.py:192
  862.1 10.7 fusion.101
  881.6 26.7 %all-reduce.1 = (f32[3,512]{1,0:T(4,128)}, f32[2048]{0:T(1024)S(1)}, f32[2048]{0:T(1024)}) all-reduce(f32[3,512]{1,0:T(4,128)S(1)} %convert_reduce_fusion.3, f32[2048]{0:T(1024)S(1)} %convert_reduce_fusion.2, f32[2048]{0:T(1024)S(1)} %copy-done.41), channel_id=1, replica_groups=mesh['dp'=8,'mp'=4] {'dp'}, use_global_device_ids=true, to_apply=%region_26.27 | all-reduce | flops 5632 | bytes 45056 | tf_op jit(solution)/shard_map/psum | solution.py:254
  908.3 39.2 %all-reduce = (f32[2048]{0:T(1024)}, f32[2048]{0:T(1024)}, f32[2048]{0:T(1024)}, f32[2048]{0:T(1024)}) all-reduce(f32[2048]{0:T(1024)S(1)} %get-tuple-element.369, f32[2048]{0:T(1024)S(1)} %get-tuple-element.370, f32[2048]{0:T(1024)S(1)} %get-tuple-element.308, ...), channel_id=1, replica_groups=mesh['dp'=8,'mp'=4] {'dp','mp'}, use_global_device_ids=true, to_apply=%region_17.18 | all-reduce | flops 8192 | bytes 65536 | tf_op jit(solution)/shard_map/psum | solution.py:281
  947.5 406.5 %all-reduce.5.cloned.1.call-done = (f32[3,2048,512]{1,2,0:T(8,128)}, f32[512,2048]{1,0:T(8,128)}, f32[2048,2048]{1,0:T(8,128)}, f32[2048,2048]{1,0:T(8,128)}) async-done(((f32[3,2048,512]{1,2,0:T(8,128)}, f32[512,2048]{1,0:T(8,128)}, f32[2048,2048]{1,0:T(8,128)}, f32[2048,2048]{1,0:T(8,128)}), (f32[3,2048,512]{1,2,0:T(8,128)}, f32[512,2048]{1,0:T(8,128)}, f32[2048,2048]{1,0:T(8,128)}, ...) | async-done | bytes 50331664 | tf_op jit(solution)/shard_map/psum | solution.py:254
  1354.0 12.7 copy.89
  1366.7 270.6 %reduce-scatter.8.cloned.1.call-done = f32[512,2048]{1,0:T(8,128)} async-done(((f32[2048,2048]{1,0:T(8,128)}), f32[512,2048]{1,0:T(8,128)}) %reduce-scatter.8.cloned.1.call-update) | async-done | bytes 4194320 | tf_op jit(solution)/shard_map/reduce_scatter | solution.py:273
  1641.2 143.7 %reduce-scatter.6.cloned.1.call-done = bf16[512,2048]{1,0:T(8,128)(2,1)} async-done(((bf16[2048,2048]{1,0:T(8,128)(2,1)}), bf16[512,2048]{1,0:T(8,128)(2,1)}) %reduce-scatter.6.cloned.1.call-update) | async-done | bytes 2097168 | tf_op jit(solution)/shard_map/reduce_scatter | solution.py:191
  1784.9 284.0 %reduce-scatter.4.cloned.1.call-done = f32[512,2048]{1,0:T(8,128)} async-done(((f32[2048,2048]{1,0:T(8,128)}), f32[512,2048]{1,0:T(8,128)}) %reduce-scatter.4.cloned.1.call-update) | async-done | bytes 4194320 | tf_op jit(solution)/shard_map/reduce_scatter | solution.py:185
  2079.6 14.0 copy.162
  (304 shorter events, 351.4 us)
Async XLA Ops:
  7.2 309.9 %copy-start = (bf16[512,2048]{1,0:T(8,128)(2,1)S(1)}, bf16[512,2048]{1,0:T(8,128)(2,1)}, u32[]{:S(2)}) copy-start(bf16[512,2048]{1,0:T(8,128)(2,1)} %param.28) | copy-start | bytes 6291460
  7.2 160.5 %all-gather.5.cloned.1.call-start = ((), (), s32[]{:S(2)}) async-start(), calls=%async_computation.3 | async-start | bytes 10485760 | tf_op jit(solution)/shard_map/all_gather | solution.py:167
  15.2 301.9 %all-gather.9.cloned.1.call-start = ((), (), s32[]{:S(2)}) async-start(), calls=%async_computation.7 | async-start | bytes 10485760 | tf_op jit(solution)/shard_map/all_gather | solution.py:202
  19.6 612.7 %all-gather.7.cloned.1.call-start = ((), (), s32[]{:S(2)}) async-start(), calls=%async_computation.5 | async-start | bytes 10485760 | tf_op jit(solution)/shard_map/all_gather | solution.py:168
  19.7 148.1 %copy-start.45 = (f32[3,512]{1,0:T(4,128)S(1)}, f32[3,512]{1,0:T(4,128)}, u32[]{:S(2)}) copy-start(f32[3,512]{1,0:T(4,128)} %param.27) | copy-start | bytes 18436
  20.3 754.6 %all-gather.11.cloned.1.call-start = ((), (), s32[]{:S(2)}) async-start(), calls=%async_computation.9 | async-start | bytes 10485760 | tf_op jit(solution)/shard_map/all_gather | solution.py:266
  20.9 1333.1 %all-reduce.5.cloned.1.call-start = ((), (), s32[]{:S(2)}) async-start(), calls=%async_computation.10 | async-start | bytes 100663296 | tf_op jit(solution)/shard_map/psum | solution.py:254
  26.6 341.3 %copy-start.12 = (f32[2048,64]{1,0:T(8,128)}, f32[2048,64]{1,0:T(8,128)S(1)}, u32[]{:S(2)}) copy-start(f32[2048,64]{1,0:T(8,128)S(1)} %get-tuple-element.391) | copy-start | bytes 1572868
  590.8 18.4 copy-start.23
  613.4 18.8 copy-start.46
  632.3 59.3 %copy-start.16 = (bf16[2048,2048]{1,0:T(8,128)(2,1)S(1)}, bf16[2048,2048]{1,0:T(8,128)(2,1)}, u32[]{:S(2)}) copy-start(bf16[2048,2048]{1,0:T(8,128)(2,1)} %all-gather.9.cloned.1.call-done) | copy-start | bytes 25165828
  632.3 59.3 %copy-start.26 = (bf16[256,8,2,256]{3,1,2,0:T(8,128)(2,1)S(1)}, bf16[256,8,2,256]{3,1,2,0:T(8,128)(2,1)}, u32[]{:S(2)}) copy-start(bf16[256,8,2,256]{3,1,2,0:T(8,128)(2,1)} %copy.120) | copy-start | bytes 6291460
  729.0 24.6 %copy-start.47 = (bf16[2048,2048]{1,0:T(8,128)(2,1)S(1)}, bf16[2048,2048]{1,0:T(8,128)(2,1)}, u32[]{:S(2)}) copy-start(bf16[2048,2048]{1,0:T(8,128)(2,1)} %get-tuple-element.362) | copy-start | bytes 25165828
  774.9 862.4 %reduce-scatter.8.cloned.1.call-start = ((), (), s32[]{:S(2)}) async-start(), calls=%async_computation.8 | async-start | bytes 20971520 | tf_op jit(solution)/shard_map/reduce_scatter | solution.py:273
  785.0 19.2 copy-start.36
  785.0 19.2 copy-start.38
  837.5 947.5 %reduce-scatter.6.cloned.1.call-start = ((), (), s32[]{:S(2)}) async-start(), calls=%async_computation.6 | async-start | bytes 10485760 | tf_op jit(solution)/shard_map/reduce_scatter | solution.py:191
  862.1 1206.9 %reduce-scatter.4.cloned.1.call-start = ((), (), s32[]{:S(2)}) async-start(), calls=%async_computation.4 | async-start | bytes 20971520 | tf_op jit(solution)/shard_map/reduce_scatter | solution.py:185
  908.3 1168.6 %copy-start.42 = (f32[2048]{0:T(1024)}, f32[2048]{0:T(1024)S(1)}, u32[]{:S(2)}) copy-start(f32[2048]{0:T(1024)S(1)} %get-tuple-element.631) | copy-start | bytes 24580
  1354.0 283.3 %copy-start.30 = (f32[512]{0:T(512)S(1)}, f32[512]{0:T(512)}, u32[]{:S(2)}) copy-start(f32[512]{0:T(512)} %copy-done.29) | copy-start | bytes 6148
  1354.0 283.3 %copy-start.32 = (f32[512]{0:T(512)S(1)}, f32[512]{0:T(512)}, u32[]{:S(2)}) copy-start(f32[512]{0:T(512)} %copy-done.31) | copy-start | bytes 6148
  1366.7 702.2 %copy-start.39 = (f32[2048]{0:T(1024)S(1)}, f32[2048]{0:T(1024)}, u32[]{:S(2)}) copy-start(f32[2048]{0:T(1024)} %param.33) | copy-start | bytes 24580
  1366.7 702.2 %copy-start.40 = (f32[2048]{0:T(1024)S(1)}, f32[2048]{0:T(1024)}, u32[]{:S(2)}) copy-start(f32[2048]{0:T(1024)} %param.29) | copy-start | bytes 24580
  1366.7 702.2 %copy-start.44 = (pred[512]{0:T(512)(128)(4,1)S(1)}, pred[512]{0:T(512)(128)(4,1)}, u32[]{:S(2)}) copy-start(pred[512]{0:T(512)(128)(4,1)} %copy-done.43) | copy-start | bytes 1540
  (51 other events, 255.3 us)
Sparse Core Ops, SparseCore 0:
  15.3 152.3 all-gather.4
  169.3 147.7 all-gather.8
  319.2 147.7 all-gather.6
  468.5 147.7 all-gather.10
  775.0 578.9 all-reduce.4
  1356.8 280.4 reduce-scatter.7
  1639.7 145.2 reduce-scatter.5
  1787.9 281.0 reduce-scatter.3
where the time goes:
time: 2110 us
  waiting for transfers between devices  1360 us (64%)
  matrix products  381 us (18%)
  local copies, waits for them, and re-layouts  164 us (8%)
  other arithmetic  115 us (5%)
  blocking collectives  65.9 us (3%)
    psum x1, waiting for transfers between devices, on_device(): lax.psum((attend_weight_grad, attend_bias_grad, merge_weight_grad, contra...  407 us
    reduce_scatter x1, waiting for transfers between devices, on_device(): lax.psum_scatter(jnp.dot(mixed, merge_weight, preferred_element_type=jnp....  284 us
    reduce_scatter x1, waiting for transfers between devices, on_device(): lax.psum_scatter(weighted, 'mp', scatter_dimension=0, tiled=True)  271 us
    reduce_scatter x1, waiting for transfers between devices, on_device(): lax.psum_scatter(jnp.dot(activated, contract_weight, preferred_element_ty...  144 us
    all_gather x1, waiting for transfers between devices, on_device(): lax.all_gather(normed_one, 'mp', axis=0, tiled=True)  141 us
    all_gather x1, waiting for transfers between devices, on_device(): full_cot = lax.all_gather(grad_out, 'mp', axis=0, tiled=True)  113 us
    unnamed x107, local copies, waits for them, and re-layouts  72.9 us
    dot_general x1, matrix products, on_device(): jnp.dot(full_two, expand_weight, preferred_element_type=jnp.float32)  59.3 us
  transfers between devices with their start and end apart: 8, of which 6 were waited for; matrix products, arithmetic and copies ran while one was open for 29% of the time, Pallas kernels for 0%

commit v1 on v0

v1 whole, which is shorter than its diff:
```python
from functools import partial

import jax
import jax.numpy as jnp
from jax import lax
from jax.experimental import pallas as pl
from jax.experimental.pallas import tpu as pltpu
from jax.sharding import PartitionSpec as P

HD = 256
ROT = 64
LANES = 128

norm_eps = 1e-05
masked_score = -1e30


def standardize(inputs):
    average = jnp.mean(inputs, axis=-1, keepdims=True)
    centred = inputs - average
    variance = jnp.mean(centred * centred, axis=-1, keepdims=True)
    inverse = lax.rsqrt(variance + norm_eps)
    return (centred * inverse, inverse)


def rotary_tables(length, rotated):
    halfway = rotated // 2
    channel = jnp.arange(halfway).astype(jnp.float32)
    frequency = 1.0 / 10000.0 ** (channel * 2.0 / rotated)
    positions = jnp.arange(length).astype(jnp.float32)
    angles = positions[:, None] * frequency[None, :]
    cosine, sine = jnp.cos(angles), jnp.sin(angles)
    rest = LANES - rotated
    ones, zeros = jnp.ones((length, rest), jnp.float32), jnp.zeros((length, rest), jnp.float32)
    none = jnp.zeros_like(sine)
    return (
        jnp.concatenate([cosine, cosine, ones], axis=1),
        jnp.concatenate([-sine, none, zeros], axis=1),
        jnp.concatenate([none, sine, zeros], axis=1),
    )


def turn_block(block, cosine, minus, plus, halfway):
    lead = block[:, :LANES]
    after = pltpu.roll(lead, LANES - halfway, 1)
    before = pltpu.roll(lead, halfway, 1)
    turned = lead * cosine + after * minus + before * plus
    return jnp.concatenate([turned, block[:, LANES:]], axis=1)


def forward_kernel(
    lengths, q_in, k_in, v_in, cos_q, min_q, plu_q, cos_k, min_k, plu_k,
    q_out, k_out, v_out, mixed_out, lse_out, *, rows, head_scale,
):
    step = pl.program_id(1)
    length = lengths[0]

    @pl.when(step == 0)
    def _():
        k_out[...] = turn_block(k_in[0], cos_k[...], min_k[...], plu_k[...], ROT // 2).astype(
            jnp.bfloat16
        )
        v_out[...] = v_in[0].astype(jnp.bfloat16)

    queries = (
        turn_block(q_in[0], cos_q[...], min_q[...], plu_q[...], ROT // 2) * head_scale
    ).astype(jnp.bfloat16)
    q_out[...] = queries

    def one_block(at, carried, diagonal):
        top, total, mixed = carried
        keys = k_out[pl.ds(at * rows, rows), :]
        values = v_out[pl.ds(at * rows, rows), :]
        scores = lax.dot_general(
            queries, keys, (((1,), (1,)), ((), ())), preferred_element_type=jnp.float32
        )
        places = lax.broadcasted_iota(jnp.int32, (rows, rows), 1)
        kept = places < length - at * rows
        if diagonal:
            kept = kept & (places <= lax.broadcasted_iota(jnp.int32, (rows, rows), 0))
        scores = jnp.where(kept, scores, masked_score)
        new_top = jnp.maximum(top, jnp.max(scores, axis=1, keepdims=True))
        shrink = jnp.exp(top - new_top)
        exponent = jnp.exp(scores - new_top)
        total = total * shrink + jnp.sum(exponent, axis=1, keepdims=True)
        mixed = mixed * shrink + lax.dot_general(
            exponent.astype(jnp.bfloat16),
            values,
            (((1,), (0,)), ((), ())),
            preferred_element_type=jnp.float32,
        )
        return (new_top, total, mixed)

    start = (
        jnp.full((rows, 1), masked_score, jnp.float32),
        jnp.zeros((rows, 1), jnp.float32),
        jnp.zeros((rows, HD), jnp.float32),
    )
    carried = lax.fori_loop(0, step, lambda at, c: one_block(at, c, False), start)
    top, total, mixed = one_block(step, carried, True)
    mixed_out[...] = (mixed / total).astype(jnp.bfloat16)
    lse_out[0] = top + jnp.log(total)


def backward_kernel(
    lengths, q_in, k_in, v_in, grad_in, mixed_in, lse_in, cosine, minus, plus,
    grads_out, key_sum, value_sum, *, rows, steps, head_scale,
):
    step = pl.program_id(1)
    length = lengths[0]

    @pl.when(step == 0)
    def _():
        key_sum[...] = jnp.zeros_like(key_sum)
        value_sum[...] = jnp.zeros_like(value_sum)

    queries = q_in[...]
    grads = grad_in[...]
    centre = jnp.sum(
        grads.astype(jnp.float32) * mixed_in[...].astype(jnp.float32), axis=1, keepdims=True
    )
    log_sum = lse_in[0]

    def one_block(at, grad_q, diagonal):
        span = pl.ds(at * rows, rows)
        keys = k_in[span, :]
        values = v_in[span, :]
        scores = lax.dot_general(
            queries, keys, (((1,), (1,)), ((), ())), preferred_element_type=jnp.float32
        )
        places = lax.broadcasted_iota(jnp.int32, (rows, rows), 1)
        kept = places < length - at * rows
        if diagonal:
            kept = kept & (places <= lax.broadcasted_iota(jnp.int32, (rows, rows), 0))
        weights = jnp.exp(jnp.where(kept, scores, masked_score) - log_sum)
        grad_w = lax.dot_general(
            grads, values, (((1,), (1,)), ((), ())), preferred_element_type=jnp.float32
        )
        grad_s = (weights * (grad_w - centre)).astype(jnp.bfloat16)
        key_sum[span, :] += lax.dot_general(
            grad_s, queries, (((0,), (0,)), ((), ())), preferred_element_type=jnp.float32
        )
        value_sum[span, :] += lax.dot_general(
            weights.astype(jnp.bfloat16),
            grads,
            (((0,), (0,)), ((), ())),
            preferred_element_type=jnp.float32,
        )
        return grad_q + lax.dot_general(
            grad_s, keys, (((1,), (0,)), ((), ())), preferred_element_type=jnp.float32
        )

    grad_q = lax.fori_loop(
        0, step, lambda at, c: one_block(at, c, False), jnp.zeros((rows, HD), jnp.float32)
    )
    grad_q = one_block(step, grad_q, True)
    here = pl.ds(step * rows, rows)
    grads_out[0, here, :] = (
        turn_block(grad_q, cosine[here, :], -minus[here, :], -plus[here, :], ROT // 2) * head_scale
    ).astype(jnp.bfloat16)

    @pl.when(step == steps - 1)
    def _():
        grads_out[1] = turn_block(
            key_sum[...], cosine[...], -minus[...], -plus[...], ROT // 2
        ).astype(jnp.bfloat16)
        grads_out[2] = value_sum[...].astype(jnp.bfloat16)


def attend_forward(projected, lengths, tables):
    _, span, width = projected.shape
    heads = width // HD
    rows = min(512, span)
    steps = span // rows
    low = jax.ShapeDtypeStruct((span, width), jnp.bfloat16)
    row_table = pl.BlockSpec((rows, LANES), lambda h, i, n: (i, 0))
    all_table = pl.BlockSpec((span, LANES), lambda h, i, n: (0, 0))
    row_block = pl.BlockSpec((rows, HD), lambda h, i, n: (i, h))
    all_block = pl.BlockSpec((span, HD), lambda h, i, n: (0, h))
    return pl.pallas_call(
        partial(forward_kernel, rows=rows, head_scale=HD ** (-0.5)),
        grid_spec=pltpu.PrefetchScalarGridSpec(
            num_scalar_prefetch=1,
            grid=(heads, steps),
            in_specs=[
                pl.BlockSpec((1, rows, HD), lambda h, i, n: (0, i, h)),
                pl.BlockSpec((1, span, HD), lambda h, i, n: (1, 0, h)),
                pl.BlockSpec((1, span, HD), lambda h, i, n: (2, 0, h)),
                row_table, row_table, row_table, all_table, all_table, all_table,
            ],
            out_specs=[
                row_block, all_block, all_block, row_block,
                pl.BlockSpec((1, rows, 1), lambda h, i, n: (h, i, 0)),
            ],
        ),
        out_shape=[low, low, low, low, jax.ShapeDtypeStruct((heads, span, 1), jnp.float32)],
        compiler_params=pltpu.CompilerParams(vmem_limit_bytes=48 * 1024 * 1024),
        name="attend_forward",
    )(lengths, projected, projected, projected, *tables, *tables)


def attend_backward(lengths, queries, keys, values, grad_mixed, mixed, lse, tables):
    span, width = queries.shape
    heads = width // HD
    rows = min(512, span)
    steps = span // rows
    all_table = pl.BlockSpec((span, LANES), lambda h, i, n: (0, 0))
    row_block = pl.BlockSpec((rows, HD), lambda h, i, n: (i, h))
    all_block = pl.BlockSpec((span, HD), lambda h, i, n: (0, h))
    return pl.pallas_call(
        partial(backward_kernel, rows=rows, steps=steps, head_scale=HD ** (-0.5)),
        grid_spec=pltpu.PrefetchScalarGridSpec(
            num_scalar_prefetch=1,
            grid=(heads, steps),
            in_specs=[
                row_block, all_block, all_block, row_block, row_block,
                pl.BlockSpec((1, rows, 1), lambda h, i, n: (h, i, 0)),
                all_table, all_table, all_table,
            ],
            out_specs=pl.BlockSpec((3, span, HD), lambda h, i, n: (0, 0, h)),
            scratch_shapes=[pltpu.VMEM((span, HD), jnp.float32)] * 2,
        ),
        out_shape=jax.ShapeDtypeStruct((3, span, width), jnp.bfloat16),
        compiler_params=pltpu.CompilerParams(vmem_limit_bytes=48 * 1024 * 1024),
        name="attend_backward",
    )(lengths, queries, keys, values, grad_mixed, mixed, lse, *tables)


def after(value, *others):
    return lax.optimization_barrier((value, *others))[0]


def on_device(
    tokens,
    lengths,
    cotangent,
    first_gain,
    first_shift,
    second_gain,
    second_shift,
    attend_weight,
    attend_bias,
    merge_weight,
    merge_bias,
    expand_weight,
    expand_bias,
    contract_weight,
    contract_bias,
):
    ring = lax.axis_size("mp")
    place = lax.axis_index("mp")
    rows_here, width = tokens.shape
    group_rows = rows_here * ring
    local_width = attend_weight.shape[2]
    local_hidden = expand_weight.shape[1]
    hops = [(i, (i + 1) % ring) for i in range(ring)]
    f32, bf16 = jnp.float32, jnp.bfloat16
    dot = partial(jnp.einsum, preferred_element_type=f32)

    def owner_row(s):
        return ((place - s) % ring) * rows_here

    def gather_ring(block):
        blocks = [block]
        for _ in range(ring - 1):
            block = lax.ppermute(block, "mp", hops)
            blocks.append(block)
        return blocks

    def in_order(blocks):
        whole = jnp.zeros((group_rows, blocks[0].shape[1]), blocks[0].dtype)
        for s, block in enumerate(blocks):
            whole = lax.dynamic_update_slice(whole, block, (owner_row(s), 0))
        return whole

    order = list(range(1, ring)) + [0]
    tables = rotary_tables(group_rows, ROT)

    token_blocks = gather_ring(tokens)
    row_ids = place * rows_here + jnp.arange(rows_here)
    valid_rows = row_ids < lengths[0]
    grad_out = jnp.where(valid_rows[:, None], cotangent, jnp.zeros_like(cotangent))
    grad_blocks = gather_ring(after(grad_out, token_blocks[-1]))

    projected = jnp.zeros((3, group_rows, local_width), f32)
    ones, twos, acts, slopes = [], [], [], []
    for s in range(ring):
        hat, _ = standardize(token_blocks[s].astype(f32))
        one = (hat * first_gain + first_shift).astype(bf16)
        two = (hat * second_gain + second_shift).astype(bf16)
        ones.append(one)
        twos.append(two)
        part = dot("td,cde->cte", one, attend_weight) + attend_bias[:, None, :]
        projected = lax.dynamic_update_slice(projected, part, (0, owner_row(s), 0))
        hidden = dot("td,df->tf", two, expand_weight) + expand_bias
        spread = 0.5 * (1.0 + lax.erf(hidden * (0.5**0.5)))
        bell = jnp.exp(-0.5 * hidden * hidden) * 0.3989422804014327
        acts.append((hidden * spread).astype(bf16))
        slopes.append((spread + hidden * bell).astype(bf16))

    queries, keys, values, mixed, lse = attend_forward(projected, lengths, tables)

    carried = None
    for s in order:
        mixed_rows = lax.dynamic_slice(mixed, (owner_row(s), 0), (rows_here, local_width))
        part = dot("tf,fd->td", mixed_rows, merge_weight)
        part = part + dot("tf,fd->td", acts[s], contract_weight)
        if carried is not None:
            part = part + carried.astype(f32)
        if s:
            send = part.astype(bf16)
            if carried is None:
                send = after(send, grad_blocks[-1])
            carried = lax.ppermute(send, "mp", hops)
    layer_output = (tokens.astype(f32) + part + merge_bias + contract_bias).astype(bf16)

    hidden_grads = []
    grad_mixed = jnp.zeros((group_rows, local_width), bf16)
    for s in range(ring):
        grad_act = dot("td,fd->tf", grad_blocks[s], contract_weight)
        hidden_grads.append((grad_act * slopes[s].astype(f32)).astype(bf16))
        rows = dot("td,fd->tf", grad_blocks[s], merge_weight).astype(bf16)
        grad_mixed = lax.dynamic_update_slice(grad_mixed, rows, (owner_row(s), 0))

    full_grad = in_order(grad_blocks)
    full_act = in_order(acts)
    full_two = in_order(twos)
    full_hidden_grad = in_order(hidden_grads)
    contract_weight_grad = dot("tf,td->fd", full_act, full_grad).astype(bf16)
    contract_weight_grad = lax.psum(contract_weight_grad, "dp")
    expand_weight_grad = dot("td,tf->df", full_two, full_hidden_grad).astype(bf16)
    expand_weight_grad = lax.psum(after(expand_weight_grad, contract_weight_grad), "dp")

    grad_projected = attend_backward(
        lengths, queries, keys, values, grad_mixed, mixed, lse, tables
    )
    merge_weight_grad = dot("tf,td->fd", mixed, full_grad).astype(bf16)
    full_one = in_order(ones)
    attend_weight_grad = dot("td,cte->cde", full_one, grad_projected).astype(bf16)
    attend_weight_grad, merge_weight_grad = lax.psum(
        (after(attend_weight_grad, expand_weight_grad), after(merge_weight_grad, expand_weight_grad)),
        "dp",
    )

    carried = None
    vectors = jnp.zeros((4, width), f32)
    for s in order:
        grads_rows = lax.dynamic_slice(
            grad_projected, (0, owner_row(s), 0), (3, rows_here, local_width)
        )
        grad_one = dot("cte,cde->td", grads_rows, attend_weight)
        grad_two = dot("tf,df->td", hidden_grads[s], expand_weight)
        hat, inverse = standardize(token_blocks[s].astype(f32))
        vectors = vectors + jnp.stack(
            [
                jnp.sum(grad_one * hat, axis=0),
                jnp.sum(grad_one, axis=0),
                jnp.sum(grad_two * hat, axis=0),
                jnp.sum(grad_two, axis=0),
            ]
        )
        part = grad_one * first_gain + grad_two * second_gain
        if carried is not None:
            part = part + carried.astype(f32)
        if s:
            carried = lax.ppermute(part.astype(bf16), "mp", hops)
    input_term = (
        part
        - jnp.mean(part, axis=-1, keepdims=True)
        - hat * jnp.mean(part * hat, axis=-1, keepdims=True)
    ) * inverse
    tokens_grad = (grad_out.astype(f32) + input_term).astype(bf16)

    own_biases = jnp.concatenate(
        [
            jnp.sum(grad_projected, axis=1, dtype=f32).reshape(-1),
            jnp.sum(full_hidden_grad, axis=0, dtype=f32),
        ]
    )
    slots = jnp.where(jnp.arange(ring)[:, None] == place, own_biases[None, :], 0.0)
    summed = lax.psum(
        jnp.concatenate(
            [vectors.reshape(-1), jnp.sum(grad_out, axis=0, dtype=f32), slots.reshape(-1)]
        ),
        ("dp", "mp"),
    )
    heads_at = 5 * width
    first_gain_grad, first_shift_grad, second_gain_grad, second_shift_grad, bias_total = (
        summed[:heads_at].reshape(5, width)
    )
    biases = lax.dynamic_slice(
        summed[heads_at:].reshape(ring, -1), (place, 0), (1, own_biases.shape[0])
    )[0]
    attend_bias_grad = biases[: 3 * local_width].reshape(3, local_width)
    expand_bias_grad = biases[3 * local_width :]
    return (
        layer_output,
        tokens_grad,
        first_gain_grad,
        first_shift_grad,
        second_gain_grad,
        second_shift_grad,
        attend_weight_grad.astype(f32),
        attend_bias_grad,
        merge_weight_grad.astype(f32),
        bias_total,
        expand_weight_grad.astype(f32),
        expand_bias_grad,
        contract_weight_grad.astype(f32),
        bias_total,
    )


def solution(mesh):
    rows = P(("dp", "mp"), None)
    columns, row_split = P(None, "mp"), P("mp", None)
    return jax.shard_map(
        on_device,
        mesh=mesh,
        in_specs=(
            rows,
            P("dp"),
            rows,
            P(),
            P(),
            P(),
            P(),
            P(None, None, "mp"),
            columns,
            row_split,
            P(),
            columns,
            P("mp"),
            row_split,
            P(),
        ),
        out_specs=(
            rows,
            rows,
            P(),
            P(),
            P(),
            P(),
            P(None, None, "mp"),
            columns,
            row_split,
            P(),
            columns,
            P("mp"),
            row_split,
            P(),
        ),
        check_vma=False,
    )
```

time: 2110 us -> 1020 us (0.48)
  waiting for transfers between devices: 1360 us -> 473 us
  local copies, waits for them, and re-layouts: 164 us -> 46.3 us
  matrix products: 381 us -> 304 us
  blocking collectives: 65.9 us -> 0 us
  Pallas kernels: 0 us -> 60.6 us
    reduce_scatter x3 -> x0, waiting for transfers between devices: 698 us -> none  [the longest x1 284 us: on_device(): lax.psum_scatter(jnp.dot(mixed, merge_weight, preferred_element_type=jnp....]
    all_gather x4 -> x0, waiting for transfers between devices: 254 us -> none  [the longest x1 141 us: on_device(): lax.all_gather(normed_one, 'mp', axis=0, tiled=True)]
    ppermute x0 -> x12, waiting for transfers between devices: none -> 148 us  [the longest x6 91.4 us: gather_ring(): block = lax.ppermute(block, 'mp', hops)]
    psum x1 -> x4, waiting for transfers between devices: 407 us -> 325 us  [the longest x1 115 us: on_device(): lax.psum((after(attend_weight_grad, expand_weight_grad), after(merge_weig...]
    dot_general x40 -> x36, matrix products: 381 us -> 304 us  [the longest x4 38.3 us: on_device(): grad_act = dot('td,fd->tf', grad_blocks[s], contract_weight)]
    psum x2 -> x0, blocking collectives: 65.9 us -> none  [the longest x1 39.2 us: on_device(): lax.psum((first_gain_grad, first_shift_grad, second_gain_grad, second_shi...]
    pallas_call x0 -> x2, Pallas kernels: none -> 60.6 us  [the longest x1 33 us: attend_backward(): pl.pallas_call(partial(backward_kernel, rows=rows, steps=steps, head_scal...]
    unnamed x107 -> x137, local copies, waits for them, and re-layouts: 72.9 us -> 16.6 us
  transfers between devices with their start and end apart: 8 -> 16, of which waited for: 6 -> 11; matrix products, arithmetic and copies ran while one was open for 29% -> 41% of each run, Pallas kernels for 0% -> 3%
where the time goes in v1:
time: 1020 us; the launch traced here: 1010 us
  waiting for transfers between devices  473 us (46%)
  matrix products  304 us (30%)
  other arithmetic  104 us (10%)
  Pallas kernels  60.6 us (6%)
  local copies, waits for them, and re-layouts  46.3 us (5%)
  between operations  15.8 us (2%)
    psum x1, waiting for transfers between devices, on_device(): lax.psum((after(attend_weight_grad, expand_weight_grad), after(merge_weig...  115 us
    ppermute x6, waiting for transfers between devices, gather_ring(): block = lax.ppermute(block, 'mp', hops)  91.4 us
    psum x1, waiting for transfers between devices, on_device(): lax.psum(jnp.concatenate([vectors.reshape(-1), jnp.sum(grad_out, axis=0,...  85.5 us
    psum x1, waiting for transfers between devices, on_device(): contract_weight_grad = lax.psum(contract_weight_grad, 'dp')  67.9 us
    psum x1, waiting for transfers between devices, on_device(): lax.psum(after(expand_weight_grad, contract_weight_grad), 'dp')  56 us
    dot_general x4, matrix products, on_device(): grad_act = dot('td,fd->tf', grad_blocks[s], contract_weight)  38.3 us
    dot_general x4, matrix products, on_device(): grad_two = dot('tf,df->td', hidden_grads[s], expand_weight)  37.9 us
    ppermute x3, waiting for transfers between devices, on_device(): carried = lax.ppermute(part.astype(bf16), 'mp', hops)  36.1 us
  transfers between devices with their start and end apart: 16, of which 11 were waited for; matrix products, arithmetic and copies ran while one was open for 41% of the time, Pallas kernels for 3%

profile of v1, /device:TPU:0, one launch (start us, length us, event | category | flops | bytes accessed | tf_op | source)
XLA Modules:
  0.0 1013.9 jit_solution(2168601375841538887)
XLA Ops:
  94.6 16.9 %collective-permute-done.1 = bf16[512,2048]{1,0:T(8,128)(2,1)S(1)} collective-permute-done((bf16[512,2048]{1,0:T(8,128)(2,1)}, bf16[512,2048]{1,0:T(8,128)(2,1)S(1)}, u32[]{:S(2)}, u32[]{:S(2)}) %collective-permute-start.1) | collective-permute-done | bytes 2097184 | tf_op jit(solution)/shard_map/ppermute | solution.py:266
  135.8 24.5 %collective-permute-done.2 = bf16[512,2048]{1,0:T(8,128)(2,1)S(1)} collective-permute-done((bf16[512,2048]{1,0:T(8,128)(2,1)S(1)}, bf16[512,2048]{1,0:T(8,128)(2,1)S(1)}, u32[]{:S(2)}, u32[]{:S(2)}) %collective-permute-start.2) | collective-permute-done | bytes 2097184 | tf_op jit(solution)/shard_map/ppermute | solution.py:266
  171.8 27.5 %attend_forward.1 = (bf16[2048,512]{1,0:T(8,128)(2,1)S(1)}, bf16[2048,512]{1,0:T(8,128)(2,1)}, bf16[2048,512]{1,0:T(8,128)(2,1)}, bf16[2048,512]{1,0:T(8,128)(2,1)}, f32[2,2048,1]{2,1,0:T(8,128)}) custom-call(s32[1]{0:T(128)} %copy.67.lengths, f32[3,2048,512]{2,1,0:T(8,128)} %bitcast_dynamic-update-slice_fusion.q_in.k_in.v_in, ...), custom_call_target="tpu_custom_call" | custom-call | tf_op jit(solution)/shard_map/attend_forward/pallas_call | solution.py:180
  215.9 10.5 %constant_dynamic-update-slice_fusion.19 = (bf16[2048,2048]{1,0:T(8,128)(2,1)S(1)}, bf16[512,2048]{1,0:T(8,128)(2,1)}) fusion(bf16[2048,2048]{1,0:T(8,128)(2,1)S(1)} %broadcast.158.clone, s32[]{:T(128)S(6)} %select_n.143, f32[512,2048]{1,0:T(8,128)} %get-tuple-element.110, f32[2048]{0:T(1024)S(1)} %copy-done.48, bf16[512,2048]{1,0:T(8,128)(2,1)} %get-tuple-element.25, ...), kind=kOutput, calls=%fused_computation.206 | convolution fusion | flops 4308598784 | bytes 18882564 | tf_op jit(solution)/shard_map/td,fd->tf/dot_general | solution.py:320
  237.5 9.6 fusion.162
  247.1 9.6 fusion.159
  281.7 22.1 %collective-permute-done.4 = bf16[512,2048]{1,0:T(8,128)(2,1)S(1)} collective-permute-done((bf16[512,2048]{1,0:T(8,128)(2,1)}, bf16[512,2048]{1,0:T(8,128)(2,1)S(1)}, u32[]{:S(2)}, u32[]{:S(2)}) %collective-permute-start.4) | collective-permute-done | bytes 2097184 | tf_op jit(solution)/shard_map/ppermute | solution.py:266
  326.1 23.7 %collective-permute-done.5 = bf16[512,2048]{1,0:T(8,128)(2,1)S(1)} collective-permute-done((bf16[512,2048]{1,0:T(8,128)(2,1)S(1)}, bf16[512,2048]{1,0:T(8,128)(2,1)S(1)}, u32[]{:S(2)}, u32[]{:S(2)}) %collective-permute-start.5) | collective-permute-done | bytes 2097184 | tf_op jit(solution)/shard_map/ppermute | solution.py:266
  353.2 33.0 %attend_backward.1 = bf16[3,2048,512]{2,1,0:T(8,128)(2,1)} custom-call(s32[1]{0:T(128)} %copy.67.lengths, bf16[2048,512]{1,0:T(8,128)(2,1)S(1)} %get-tuple-element.27.q_in, bf16[2048,512]{1,0:T(8,128)(2,1)} %get-tuple-element.28.k_in, bf16[2048,512]{1,0:T(8,128)(2,1)} %get-tuple-element.29.v_in, bf16[2048,512]{1,0:T(8,128)(2,1)} %fusion.119.grad_in, ...), custom_call_target="tpu_custom_call" | custom-call | tf_op jit(solution)/shard_map/attend_backward/pallas_call | solution.py:210
  386.3 10.8 %fusion.58 = (f32[2048]{0:T(1024)S(1)}, f32[2048]{0:T(1024)S(1)}, f32[2048]{0:T(1024)S(1)}, f32[2048]{0:T(1024)S(1)}, bf16[512,2048]{1,0:T(8,128)(2,1)}) fusion(bf16[512,2048]{1,0:T(8,128)(2,1)} %collective-permute-done, f32[512]{0:T(512)S(1)} %copy-done.45, f32[512]{0:T(512)S(1)} %copy-done.41, f32[512,2048]{1,0:T(8,128)} %fusion.165, ...), kind=kOutput, calls=%fused_computation.76 | convolution fusion | flops 3234848768 | bytes 16306180 | tf_op jit(solution)/shard_map/cte,cde->td/dot_general | solution.py:351
  397.2 9.8 constant_dynamic-update-slice_fusion.16
  410.3 18.0 %convert_bitcast_fusion = bf16[3,2048,512]{1,2,0:T(8,128)(2,1)} fusion(bf16[3,2048,512]{2,1,0:T(8,128)(2,1)S(1)} %bitcast.150, bf16[2048,2048]{1,0:T(8,128)(2,1)} %get-tuple-element.93), kind=kOutput, calls=%fused_computation.6 | convolution fusion | flops 12888047616 | bytes 20971520 | tf_op jit(solution)/shard_map/td,cte->cde/dot_general | solution.py:339
  429.7 24.1 %convolution_convert_fusion = bf16[2048,2048]{1,0:T(8,128)(2,1)} fusion(bf16[2048,2048]{1,0:T(8,128)(2,1)} %get-tuple-element.78, bf16[2048,2048]{1,0:T(8,128)(2,1)} %constant_dynamic-update-slice_fusion), kind=kOutput, calls=%fused_computation.4 | convolution fusion | flops 17184063488 | bytes 25165824 | tf_op jit(solution)/shard_map/tf,td->fd/dot_general | solution.py:329
  453.9 23.7 %convolution_convert_fusion.1 = bf16[2048,2048]{1,0:T(8,128)(2,1)} fusion(bf16[2048,2048]{1,0:T(8,128)(2,1)} %get-tuple-element.92, bf16[2048,2048]{1,0:T(8,128)(2,1)} %copy-done.4), kind=kOutput, calls=%fused_computation.5 | convolution fusion | flops 17184063488 | bytes 25165824 | tf_op jit(solution)/shard_map/td,tf->df/dot_general | solution.py:331
  513.3 67.9 %all-reduce.8.cloned.1.call-done = bf16[2048,2048]{1,0:T(8,128)(2,1)} async-done(((bf16[2048,2048]{1,0:T(8,128)(2,1)}), bf16[2048,2048]{1,0:T(8,128)(2,1)}) %all-reduce.8.cloned.1.call-update) | async-done | bytes 8388624 | tf_op jit(solution)/shard_map/psum | solution.py:330
  602.7 36.1 %collective-permute-done.11 = bf16[512,2048]{1,0:T(8,128)(2,1)} collective-permute-done((bf16[512,2048]{1,0:T(8,128)(2,1)}, bf16[512,2048]{1,0:T(8,128)(2,1)}, u32[]{:S(2)}, u32[]{:S(2)}) %collective-permute-start.11) | collective-permute-done | bytes 2097184 | tf_op jit(solution)/shard_map/ppermute | solution.py:366
  645.7 10.0 convolution_convert_fusion.2
  655.7 56.0 %all-reduce.10.cloned.1.call-done = bf16[2048,2048]{1,0:T(8,128)(2,1)} async-done(((bf16[2048,2048]{1,0:T(8,128)(2,1)}), bf16[2048,2048]{1,0:T(8,128)(2,1)}) %all-reduce.10.cloned.1.call-update) | async-done | bytes 8388624 | tf_op jit(solution)/shard_map/psum | solution.py:332
  720.0 10.5 %fusion.158 = f32[512,2048]{1,0:T(8,128)} fusion(bf16[512,2048]{1,0:T(8,128)(2,1)} %get-tuple-element.85, bf16[2048,2048]{1,0:T(8,128)(2,1)} %param.28), kind=kOutput, calls=%fused_computation.236 | convolution fusion | flops 4294967296 | bytes 14680064 | tf_op jit(solution)/shard_map/tf,fd->td/dot_general | solution.py:307
  734.9 11.8 %convert_element_type.265 = f32[2048,2048]{1,0:T(8,128)} convert(bf16[2048,2048]{1,0:T(8,128)(2,1)} %all-reduce.8.cloned.1.call-done) | non-fusion elementwise | flops 4194304 | bytes 25165824 | tf_op jit(solution)/shard_map/convert_element_type | solution.py:409
  746.7 20.9 %collective-permute-done.8 = bf16[512,2048]{1,0:T(8,128)(2,1)} collective-permute-done((bf16[512,2048]{1,0:T(8,128)(2,1)}, bf16[512,2048]{1,0:T(8,128)(2,1)}, u32[]{:S(2)}, u32[]{:S(2)}) %collective-permute-start.8) | collective-permute-done | bytes 2097184 | tf_op jit(solution)/shard_map/ppermute | solution.py:314
  776.5 85.5 %all-reduce.6.cloned.1.call-done = f32[24576]{0:T(1024)} async-done(((f32[24576]{0:T(1024)}), f32[24576]{0:T(1024)}) %all-reduce.6.cloned.1.call-update) | async-done | bytes 98320 | tf_op jit(solution)/shard_map/psum | solution.py:381
  865.6 11.9 %convert_element_type.264 = f32[2048,2048]{1,0:T(8,128)} convert(bf16[2048,2048]{1,0:T(8,128)(2,1)} %all-reduce.10.cloned.1.call-done) | non-fusion elementwise | flops 4194304 | bytes 25165824 | tf_op jit(solution)/shard_map/convert_element_type | solution.py:407
  877.5 115.3 %all-reduce.12.cloned.1.call-done = (bf16[3,2048,512]{1,2,0:T(8,128)(2,1)}, bf16[512,2048]{1,0:T(8,128)(2,1)}) async-done(((bf16[3,2048,512]{1,2,0:T(8,128)(2,1)}, bf16[512,2048]{1,0:T(8,128)(2,1)}), (bf16[3,2048,512]{1,2,0:T(8,128)(2,1)}, bf16[512,2048]{1,0:T(8,128)(2,1)})) %all-reduce.12.cloned.1.call-update) | async-done | bytes 8388624 | tf_op jit(solution)/shard_map/psum | solution.py:340
  (263 shorter events, 308.2 us)
Async XLA Ops:
  7.2 155.7 %copy-start = (bf16[512,2048]{1,0:T(8,128)(2,1)S(1)}, bf16[512,2048]{1,0:T(8,128)(2,1)}, u32[]{:S(2)}) copy-start(bf16[512,2048]{1,0:T(8,128)(2,1)} %param.24) | copy-start | bytes 6291460
  7.2 574.1 %all-reduce.8.cloned.1.call-start = ((), (), s32[]{:S(2)}) async-start(), calls=%async_computation.1 | async-start | bytes 16777216 | tf_op jit(solution)/shard_map/psum | solution.py:330
  7.2 51.1 %collective-permute-start = (bf16[512,2048]{1,0:T(8,128)(2,1)}, bf16[512,2048]{1,0:T(8,128)(2,1)}, u32[]{:S(2)}, u32[]{:S(2)}) collective-permute-start(bf16[512,2048]{1,0:T(8,128)(2,1)} %param.15), channel_id=1, source_target_pairs={{0,1},{1,2},{2,3},{3,0},{4,5},{5,6},{6,7},{7,4},{8,9},{9,10},{10,1... | collective-permute-start | bytes 6291464 | tf_op jit(solution)/shard_map/ppermute | solution.py:266
  62.6 48.9 %collective-permute-start.1 = (bf16[512,2048]{1,0:T(8,128)(2,1)}, bf16[512,2048]{1,0:T(8,128)(2,1)S(1)}, u32[]{:S(2)}, u32[]{:S(2)}) collective-permute-start(bf16[512,2048]{1,0:T(8,128)(2,1)} %collective-permute-done), channel_id=1, source_target_pairs={{0,1},{1,2},{2,3},{3,0},{4,5},{5,6},{6,7},{7,4},{8,9},{9,10},{10,1... | collective-permute-start | bytes 6291464 | tf_op jit(solution)/shard_map/ppermute | solution.py:266
  112.5 47.8 %collective-permute-start.2 = (bf16[512,2048]{1,0:T(8,128)(2,1)S(1)}, bf16[512,2048]{1,0:T(8,128)(2,1)S(1)}, u32[]{:S(2)}, u32[]{:S(2)}) collective-permute-start(bf16[512,2048]{1,0:T(8,128)(2,1)S(1)} %collective-permute-done.1), channel_id=1, source_target_pairs={{0,1},{1,2},{2,3},{3,0},{4,5},{5,6},{6,7},{7,4},{8,9},{9,10},{10,1... | collective-permute-start | bytes 6291464 | tf_op jit(solution)/shard_map/ppermute | solution.py:266
  124.3 42.3 %slice-start.12 = ((s8[6291456]{0:T(1024)(128)(4,1)}), s8[4194304]{0:T(1024)(128)(4,1)S(1)}, s32[]{:S(2)}) async-start(s8[6291456]{0:T(1024)(128)(4,1)} %bitcast.179), calls=%async_computation.16 | async-start | bytes 8388608
  160.7 73.4 %copy-start.32 = (f32[512]{0:T(512)}, f32[512]{0:T(512)S(1)}, u32[]{:S(2)}) copy-start(f32[512]{0:T(512)S(1)} %broadcast_multiply_fusion.2) | copy-start | bytes 6148
  161.4 72.7 %copy-start.36 = (f32[512]{0:T(512)}, f32[512]{0:T(512)S(1)}, u32[]{:S(2)}) copy-start(f32[512]{0:T(512)S(1)} %add_rsqrt_fusion) | copy-start | bytes 6148
  161.4 95.3 %collective-permute-start.3 = (bf16[512,2048]{1,0:T(8,128)(2,1)}, bf16[512,2048]{1,0:T(8,128)(2,1)}, u32[]{:S(2)}, u32[]{:S(2)}) collective-permute-start(bf16[512,2048]{1,0:T(8,128)(2,1)} %get-tuple-element.25), channel_id=1, source_target_pairs={{0,1},{1,2},{2,3},{3,0},{4,5},{5,6},{6,7},{7,4},{8,9},{9,10},{10,1... | collective-permute-start | bytes 6291464 | tf_op jit(solution)/shard_map/ppermute | solution.py:266
  256.7 47.1 %collective-permute-start.4 = (bf16[512,2048]{1,0:T(8,128)(2,1)}, bf16[512,2048]{1,0:T(8,128)(2,1)S(1)}, u32[]{:S(2)}, u32[]{:S(2)}) collective-permute-start(bf16[512,2048]{1,0:T(8,128)(2,1)} %collective-permute-done.3), channel_id=1, source_target_pairs={{0,1},{1,2},{2,3},{3,0},{4,5},{5,6},{6,7},{7,4},{8,9},{9,10},{10,1... | collective-permute-start | bytes 6291464 | tf_op jit(solution)/shard_map/ppermute | solution.py:266
  303.8 46.0 %collective-permute-start.5 = (bf16[512,2048]{1,0:T(8,128)(2,1)S(1)}, bf16[512,2048]{1,0:T(8,128)(2,1)S(1)}, u32[]{:S(2)}, u32[]{:S(2)}) collective-permute-start(bf16[512,2048]{1,0:T(8,128)(2,1)S(1)} %collective-permute-done.4), channel_id=1, source_target_pairs={{0,1},{1,2},{2,3},{3,0},{4,5},{5,6},{6,7},{7,4},{8,9},{9,10},{10,1... | collective-permute-start | bytes 6291464 | tf_op jit(solution)/shard_map/ppermute | solution.py:266
  397.1 87.0 %collective-permute-start.9 = (bf16[512,2048]{1,0:T(8,128)(2,1)}, bf16[512,2048]{1,0:T(8,128)(2,1)}, u32[]{:S(2)}, u32[]{:S(2)}) collective-permute-start(bf16[512,2048]{1,0:T(8,128)(2,1)} %get-tuple-element.91), channel_id=1, source_target_pairs={{0,1},{1,2},{2,3},{3,0},{4,5},{5,6},{6,7},{7,4},{8,9},{9,10},{10,1... | collective-permute-start | bytes 6291464 | tf_op jit(solution)/shard_map/ppermute | solution.py:366
  397.1 199.7 %collective-permute-start.6 = (bf16[512,2048]{1,0:T(8,128)(2,1)}, bf16[512,2048]{1,0:T(8,128)(2,1)}, u32[]{:S(2)}, u32[]{:S(2)}) collective-permute-start(bf16[512,2048]{1,0:T(8,128)(2,1)} %add_convert_fusion.2), channel_id=1, source_target_pairs={{0,1},{1,2},{2,3},{3,0},{4,5},{5,6},{6,7},{7,4},{8,9},{9,10},{10,1... | collective-permute-start | bytes 6291464 | tf_op jit(solution)/shard_map/ppermute | solution.py:314
  453.8 257.9 %all-reduce.10.cloned.1.call-start = ((), (), s32[]{:S(2)}) async-start(), calls=%async_computation.2 | async-start | bytes 16777216 | tf_op jit(solution)/shard_map/psum | solution.py:332
  489.2 92.2 %collective-permute-start.10 = (bf16[512,2048]{1,0:T(8,128)(2,1)}, bf16[512,2048]{1,0:T(8,128)(2,1)}, u32[]{:S(2)}, u32[]{:S(2)}) collective-permute-start(bf16[512,2048]{1,0:T(8,128)(2,1)} %get-tuple-element.90), channel_id=1, source_target_pairs={{0,1},{1,2},{2,3},{3,0},{4,5},{5,6},{6,7},{7,4},{8,9},{9,10},{10,1... | collective-permute-start | bytes 6291464 | tf_op jit(solution)/shard_map/ppermute | solution.py:366
  513.3 68.0 %copy-start.33 = (f32[512]{0:T(512)S(1)}, f32[512]{0:T(512)}, u32[]{:S(2)}) copy-start(f32[512]{0:T(512)} %copy-done.32) | copy-start | bytes 6148
  513.3 68.0 %copy-start.37 = (f32[512]{0:T(512)S(1)}, f32[512]{0:T(512)}, u32[]{:S(2)}) copy-start(f32[512]{0:T(512)} %copy-done.36) | copy-start | bytes 6148
  581.3 280.7 %all-reduce.6.cloned.1.call-start = ((), (), s32[]{:S(2)}) async-start(), calls=%async_computation | async-start | bytes 196608 | tf_op jit(solution)/shard_map/psum | solution.py:381
  588.2 50.6 %collective-permute-start.11 = (bf16[512,2048]{1,0:T(8,128)(2,1)}, bf16[512,2048]{1,0:T(8,128)(2,1)}, u32[]{:S(2)}, u32[]{:S(2)}) collective-permute-start(bf16[512,2048]{1,0:T(8,128)(2,1)} %get-tuple-element.89), channel_id=1, source_target_pairs={{0,1},{1,2},{2,3},{3,0},{4,5},{5,6},{6,7},{7,4},{8,9},{9,10},{10,1... | collective-permute-start | bytes 6291464 | tf_op jit(solution)/shard_map/ppermute | solution.py:366
  601.2 43.6 %copy-start.30 = (f32[2048]{0:T(1024)S(1)}, f32[2048]{0:T(1024)}, u32[]{:S(2)}) copy-start(f32[2048]{0:T(1024)} %get-tuple-element.86) | copy-start | bytes 24580
  601.2 113.0 %collective-permute-start.7 = (bf16[512,2048]{1,0:T(8,128)(2,1)}, bf16[512,2048]{1,0:T(8,128)(2,1)}, u32[]{:S(2)}, u32[]{:S(2)}) collective-permute-start(bf16[512,2048]{1,0:T(8,128)(2,1)} %add_convert_fusion.1), channel_id=1, source_target_pairs={{0,1},{1,2},{2,3},{3,0},{4,5},{5,6},{6,7},{7,4},{8,9},{9,10},{10,1... | collective-permute-start | bytes 6291464 | tf_op jit(solution)/shard_map/ppermute | solution.py:314
  645.4 347.3 %all-reduce.12.cloned.1.call-start = ((), (), s32[]{:S(2)}) async-start(), calls=%async_computation.3 | async-start | bytes 16777216 | tf_op jit(solution)/shard_map/psum | solution.py:340
  718.3 49.3 %collective-permute-start.8 = (bf16[512,2048]{1,0:T(8,128)(2,1)}, bf16[512,2048]{1,0:T(8,128)(2,1)}, u32[]{:S(2)}, u32[]{:S(2)}) collective-permute-start(bf16[512,2048]{1,0:T(8,128)(2,1)} %add_convert_fusion), channel_id=1, source_target_pairs={{0,1},{1,2},{2,3},{3,0},{4,5},{5,6},{6,7},{7,4},{8,9},{9,10},{10,1... | collective-permute-start | bytes 6291464 | tf_op jit(solution)/shard_map/ppermute | solution.py:314
  865.6 140.7 %copy-start.31 = (f32[2048]{0:T(1024)}, f32[2048]{0:T(1024)S(1)}, u32[]{:S(2)}) copy-start(f32[2048]{0:T(1024)S(1)} %get-tuple-element.150) | copy-start | bytes 24580
  (59 other events, 853.3 us)
Sparse Core Ops, SparseCore 0:
  453.9 127.3 all-reduce.7
  585.3 126.3 all-reduce.9
  717.3 144.7 all-reduce.5
  865.6 127.0 all-reduce.11

commit v2 on v1

--- a/solution.py
+++ b/solution.py
@@ -230,6 +230,49 @@
     return lax.optimization_barrier((value, *others))[0]
 
 
+def xor_sum(vector, axis):
+    size = lax.axis_size(axis)
+    bit = 1
+    while bit < size:
+        vector = vector + lax.ppermute(vector, axis, [(i, i ^ bit) for i in range(size)])
+        bit *= 2
+    return vector
+
+
+def cube_sum(array):
+    size = lax.axis_size("dp")
+    index = lax.axis_index("dp")
+    bits = [1 << k for k in range(size.bit_length() - 1)]
+
+    def exchange(value, bit):
+        return lax.ppermute(value, "dp", [(i, i ^ bit) for i in range(size)])
+
+    def halve(value, bit):
+        half = value.shape[0] // 2
+        side = (index // bit) % 2
+        kept = lax.dynamic_slice_in_dim(value, side * half, half, 0)
+        sent = lax.dynamic_slice_in_dim(value, (1 - side) * half, half, 0)
+        got = exchange(sent, bit)
+        return (kept.astype(jnp.float32) + got.astype(jnp.float32)).astype(value.dtype)
+
+    def restore(value, bit):
+        got = exchange(value, bit)
+        upper = (index // bit) % 2 == 1
+        return (jnp.where(upper, got, value), jnp.where(upper, value, got))
+
+    array = halve(array, bits[0])
+    middle = array.shape[0] // 2
+    parts = []
+    for part, order in ((array[:middle], bits[1:]), (array[middle:], bits[2:] + bits[1:2])):
+        for bit in order:
+            part = halve(part, bit)
+        for bit in reversed(order):
+            part = jnp.concatenate(restore(part, bit), axis=0)
+        parts.append(part)
+    whole = restore(jnp.concatenate(parts, axis=0), bits[0])
+    return jnp.concatenate([half.astype(jnp.float32) for half in whole], axis=0)
+
+
 def on_device(
     tokens,
     lengths,
@@ -252,147 +295,154 @@
     rows_here, width = tokens.shape
     group_rows = rows_here * ring
     local_width = attend_weight.shape[2]
-    local_hidden = expand_weight.shape[1]
-    hops = [(i, (i + 1) % ring) for i in range(ring)]
     f32, bf16 = jnp.float32, jnp.bfloat16
     dot = partial(jnp.einsum, preferred_element_type=f32)
+    up = [(i, (i + 1) % ring) for i in range(ring)]
+    down = [(i, (i - 1) % ring) for i in range(ring)]
+    up_hops = ring // 2
+    down_hops = ring - 1 - up_hops
 
     def owner_row(s):
         return ((place - s) % ring) * rows_here
 
-    def gather_ring(block):
-        blocks = [block]
-        for _ in range(ring - 1):
-            block = lax.ppermute(block, "mp", hops)
-            blocks.append(block)
+    def gather_blocks(block):
+        blocks = {0: block}
+        for s in range(1, up_hops + 1):
+            blocks[s] = lax.ppermute(blocks[s - 1], "mp", up)
+        for s in range(1, down_hops + 1):
+            blocks[ring - s] = lax.ppermute(blocks[(ring - s + 1) % ring], "mp", down)
         return blocks
+
+    arrival = [0]
+    for s in range(1, up_hops + 1):
+        arrival += [s] + ([ring - s] if s <= down_hops else [])
+
+    def scatter_blocks(part_of, first_after=()):
+        total = part_of(0)
+        for hops, count, sign in ((up, up_hops, -1), (down, down_hops, 1)):
+            carried = None
+            for k in range(count, 0, -1):
+                part = part_of(sign * k % ring)
+                if carried is not None:
+                    part = part + carried.astype(f32)
+                part = part.astype(bf16)
+                if carried is None and first_after:
+                    part = after(part, *first_after)
+                carried = lax.ppermute(part, "mp", hops)
+            if carried is not None:
+                total = total + carried.astype(f32)
+        return total
 
     def in_order(blocks):
         whole = jnp.zeros((group_rows, blocks[0].shape[1]), blocks[0].dtype)
-        for s, block in enumerate(blocks):
-            whole = lax.dynamic_update_slice(whole, block, (owner_row(s), 0))
+        for s in arrival:
+            whole = lax.dynamic_update_slice(whole, blocks[s], (owner_row(s), 0))
         return whole
 
-    order = list(range(1, ring)) + [0]
     tables = rotary_tables(group_rows, ROT)
 
-    token_blocks = gather_ring(tokens)
+    token_blocks = gather_blocks(tokens)
     row_ids = place * rows_here + jnp.arange(rows_here)
     valid_rows = row_ids < lengths[0]
     grad_out = jnp.where(valid_rows[:, None], cotangent, jnp.zeros_like(cotangent))
-    grad_blocks = gather_ring(after(grad_out, token_blocks[-1]))
+    grad_blocks = gather_blocks(after(grad_out, token_blocks[1], token_blocks[ring - 1]))
 
     projected = jnp.zeros((3, group_rows, local_width), f32)
-    ones, twos, acts, slopes = [], [], [], []
-    for s in range(ring):
+    ones, twos, acts, slopes = {}, {}, {}, {}
+    for s in arrival:
         hat, _ = standardize(token_blocks[s].astype(f32))
-        one = (hat * first_gain + first_shift).astype(bf16)
-        two = (hat * second_gain + second_shift).astype(bf16)
-        ones.append(one)
-        twos.append(two)
-        part = dot("td,cde->cte", one, attend_weight) + attend_bias[:, None, :]
+        ones[s] = (hat * first_gain + first_shift).astype(bf16)
+        twos[s] = (hat * second_gain + second_shift).astype(bf16)
+        part = dot("td,cde->cte", ones[s], attend_weight) + attend_bias[:, None, :]
         projected = lax.dynamic_update_slice(projected, part, (0, owner_row(s), 0))
-        hidden = dot("td,df->tf", two, expand_weight) + expand_bias
+        hidden = dot("td,df->tf", twos[s], expand_weight) + expand_bias
         spread = 0.5 * (1.0 + lax.erf(hidden * (0.5**0.5)))
         bell = jnp.exp(-0.5 * hidden * hidden) * 0.3989422804014327
-        acts.append((hidden * spread).astype(bf16))
-        slopes.append((spread + hidden * bell).astype(bf16))
+        acts[s] = (hidden * spread).astype(bf16)
+        slopes[s] = (spread + hidden * bell).astype(bf16)
 
     queries, keys, values, mixed, lse = attend_forward(projected, lengths, tables)
 
-    carried = None
-    for s in order:
-        mixed_rows = lax.dynamic_slice(mixed, (owner_row(s), 0), (rows_here, local_width))
-        part = dot("tf,fd->td", mixed_rows, merge_weight)
-        part = part + dot("tf,fd->td", acts[s], contract_weight)
-        if carried is not None:
-            part = part + carried.astype(f32)
-        if s:
-            send = part.astype(bf16)
-            if carried is None:
-                send = after(send, grad_blocks[-1])
-            carried = lax.ppermute(send, "mp", hops)
-    layer_output = (tokens.astype(f32) + part + merge_bias + contract_bias).astype(bf16)
-
-    hidden_grads = []
+    hidden_grads = {}
     grad_mixed = jnp.zeros((group_rows, local_width), bf16)
-    for s in range(ring):
+    for s in arrival:
         grad_act = dot("td,fd->tf", grad_blocks[s], contract_weight)
-        hidden_grads.append((grad_act * slopes[s].astype(f32)).astype(bf16))
+        hidden_grads[s] = (grad_act * slopes[s].astype(f32)).astype(bf16)
         rows = dot("td,fd->tf", grad_blocks[s], merge_weight).astype(bf16)
         grad_mixed = lax.dynamic_update_slice(grad_mixed, rows, (owner_row(s), 0))
 
     full_grad = in_order(grad_blocks)
-    full_act = in_order(acts)
-    full_two = in_order(twos)
     full_hidden_grad = in_order(hidden_grads)
-    contract_weight_grad = dot("tf,td->fd", full_act, full_grad).astype(bf16)
-    contract_weight_grad = lax.psum(contract_weight_grad, "dp")
-    expand_weight_grad = dot("td,tf->df", full_two, full_hidden_grad).astype(bf16)
-    expand_weight_grad = lax.psum(after(expand_weight_grad, contract_weight_grad), "dp")
+    contract_weight_grad = dot("tf,td->fd", in_order(acts), full_grad).astype(bf16)
+    expand_weight_grad = dot("td,tf->df", in_order(twos), full_hidden_grad).astype(bf16)
+    merge_weight_grad = dot("tf,td->fd", mixed, full_grad).astype(bf16)
+    grad_mixed = after(grad_mixed, contract_weight_grad, expand_weight_grad)
+    contract_weight_grad = cube_sum(contract_weight_grad)
+    expand_weight_grad = cube_sum(expand_weight_grad)
+    merge_weight_grad = cube_sum(merge_weight_grad)
+
+    def branch_part(s):
+        mixed_rows = lax.dynamic_slice(mixed, (owner_row(s), 0), (rows_here, local_width))
+        return dot("tf,fd->td", mixed_rows, merge_weight) + dot(
+            "tf,fd->td", acts[s], contract_weight
+        )
+
+    branches = scatter_blocks(branch_part, (grad_blocks[up_hops],))
+    layer_output = (tokens.astype(f32) + branches + merge_bias + contract_bias).astype(bf16)
 
     grad_projected = attend_backward(
         lengths, queries, keys, values, grad_mixed, mixed, lse, tables
     )
-    merge_weight_grad = dot("tf,td->fd", mixed, full_grad).astype(bf16)
-    full_one = in_order(ones)
-    attend_weight_grad = dot("td,cte->cde", full_one, grad_projected).astype(bf16)
-    attend_weight_grad, merge_weight_grad = lax.psum(
-        (after(attend_weight_grad, expand_weight_grad), after(merge_weight_grad, expand_weight_grad)),
-        "dp",
-    )
-
-    carried = None
-    vectors = jnp.zeros((4, width), f32)
-    for s in order:
+    attend_weight_grad = dot("td,cte->cde", in_order(ones), grad_projected).astype(bf16)
+    attend_weight_grad = cube_sum(attend_weight_grad.reshape(3 * width, local_width))
+
+    vectors = []
+
+    def normed_part(s):
         grads_rows = lax.dynamic_slice(
             grad_projected, (0, owner_row(s), 0), (3, rows_here, local_width)
         )
         grad_one = dot("cte,cde->td", grads_rows, attend_weight)
         grad_two = dot("tf,df->td", hidden_grads[s], expand_weight)
-        hat, inverse = standardize(token_blocks[s].astype(f32))
-        vectors = vectors + jnp.stack(
-            [
-                jnp.sum(grad_one * hat, axis=0),
-                jnp.sum(grad_one, axis=0),
-                jnp.sum(grad_two * hat, axis=0),
-                jnp.sum(grad_two, axis=0),
-            ]
-        )
-        part = grad_one * first_gain + grad_two * second_gain
-        if carried is not None:
-            part = part + carried.astype(f32)
-        if s:
-            carried = lax.ppermute(part.astype(bf16), "mp", hops)
+        hat, _ = standardize(token_blocks[s].astype(f32))
+        vectors.append(
+            jnp.stack(
+                [
+                    jnp.sum(grad_one * hat, axis=0),
+                    jnp.sum(grad_one, axis=0),
+                    jnp.sum(grad_two * hat, axis=0),
+                    jnp.sum(grad_two, axis=0),
+                ]
+            )
+        )
+        return grad_one * first_gain + grad_two * second_gain
+
+    weighted = scatter_blocks(normed_part)
+    hat, inverse = standardize(tokens.astype(f32))
     input_term = (
-        part
-        - jnp.mean(part, axis=-1, keepdims=True)
-        - hat * jnp.mean(part * hat, axis=-1, keepdims=True)
+        weighted
+        - jnp.mean(weighted, axis=-1, keepdims=True)
+        - hat * jnp.mean(weighted * hat, axis=-1, keepdims=True)
     ) * inverse
     tokens_grad = (grad_out.astype(f32) + input_term).astype(bf16)
 
-    own_biases = jnp.concatenate(
+    summed = jnp.concatenate(
         [
+            sum(vectors).reshape(-1),
+            jnp.sum(grad_out, axis=0, dtype=f32),
             jnp.sum(grad_projected, axis=1, dtype=f32).reshape(-1),
             jnp.sum(full_hidden_grad, axis=0, dtype=f32),
         ]
     )
-    slots = jnp.where(jnp.arange(ring)[:, None] == place, own_biases[None, :], 0.0)
-    summed = lax.psum(
-        jnp.concatenate(
-            [vectors.reshape(-1), jnp.sum(grad_out, axis=0, dtype=f32), slots.reshape(-1)]
-        ),
-        ("dp", "mp"),
-    )
+    summed = xor_sum(summed, "dp")
     heads_at = 5 * width
-    first_gain_grad, first_shift_grad, second_gain_grad, second_shift_grad, bias_total = (
-        summed[:heads_at].reshape(5, width)
-    )
-    biases = lax.dynamic_slice(
-        summed[heads_at:].reshape(ring, -1), (place, 0), (1, own_biases.shape[0])
-    )[0]
+    first_gain_grad, first_shift_grad, second_gain_grad, second_shift_grad, bias_total = xor_sum(
+        summed[:heads_at], "mp"
+    ).reshape(5, width)
+    biases = summed[heads_at:]
     attend_bias_grad = biases[: 3 * local_width].reshape(3, local_width)
     expand_bias_grad = biases[3 * local_width :]
+    attend_weight_grad = attend_weight_grad.reshape(attend_weight.shape)
     return (
         layer_output,
         tokens_grad,
@@ -400,13 +450,13 @@
         first_shift_grad,
         second_gain_grad,
         second_shift_grad,
-        attend_weight_grad.astype(f32),
+        attend_weight_grad,
         attend_bias_grad,
-        merge_weight_grad.astype(f32),
+        merge_weight_grad,
         bias_total,
-        expand_weight_grad.astype(f32),
+        expand_weight_grad,
         expand_bias_grad,
-        contract_weight_grad.astype(f32),
+        contract_weight_grad,
         bias_total,
     )
 

time: 1020 us -> 1010 us (level)
  waiting for transfers between devices: 473 us -> 353 us
  other arithmetic: 104 us -> 152 us
  starting transfers between devices: 10.2 us -> 57.9 us
  local copies, waits for them, and re-layouts: 46.3 us -> 71.2 us
  between operations: 15.8 us -> 3.83 us
    psum x4 -> x0, waiting for transfers between devices: 325 us -> none  [the longest x1 115 us: on_device(): lax.psum((after(attend_weight_grad, expand_weight_grad), after(merge_weig...]
    ppermute x12 -> x57, waiting for transfers between devices: 148 us -> 353 us  [the longest x40 209 us: exchange(): return lax.ppermute(value, 'dp', [(i, i ^ bit) for i in range(size)])]
    ppermute x12 -> x57, starting transfers between devices: 9.87 us -> 57.9 us  [the longest x40 42.6 us: exchange(): return lax.ppermute(value, 'dp', [(i, i ^ bit) for i in range(size)])]
    concatenate x2 -> x18, other arithmetic: 0.65 us -> 38.2 us  [the longest x4 28.6 us: cube_sum(): return jnp.concatenate([half.astype(jnp.float32) for half in whole], axis=0)]
    select_n x1 -> x19, other arithmetic: 0.08 us -> 19.6 us  [restore(): return (jnp.where(upper, got, value), jnp.where(upper, value, got))]
    dynamic_slice x0 -> x20, local copies, waits for them, and re-layouts: none -> 14.7 us  [halve(): sent = lax.dynamic_slice_in_dim(value, (1 - side) * half, half, 0)]
    convert_element_type x5 -> x21, other arithmetic: 36.3 us -> 23.5 us  [the longest x20 19.2 us: halve(): (kept.astype(jnp.float32) + got.astype(jnp.float32)).astype(value.dtype)]
  transfers between devices with their start and end apart: 16 -> 57, of which waited for: 11 -> 27; matrix products, arithmetic and copies ran while one was open for 41% -> 38% of each run, Pallas kernels for 3% -> 3%
where the time goes in v2:
time: 1010 us; the launch traced here: 1000 us
  waiting for transfers between devices  353 us (35%)
  matrix products  304 us (30%)
  other arithmetic  152 us (15%)
  local copies, waits for them, and re-layouts  71.2 us (7%)
  Pallas kernels  60.6 us (6%)
  starting transfers between devices  57.9 us (6%)
    ppermute x40, waiting for transfers between devices, exchange(): return lax.ppermute(value, 'dp', [(i, i ^ bit) for i in range(size)])  209 us
    ppermute x6, waiting for transfers between devices, scatter_blocks(): carried = lax.ppermute(part, 'mp', hops)  64.9 us
    ppermute x40, starting transfers between devices, exchange(): return lax.ppermute(value, 'dp', [(i, i ^ bit) for i in range(size)])  42.6 us
    dot_general x4, matrix products, on_device(): hidden = dot('td,df->tf', twos[s], expand_weight) + expand_bias  39.8 us
    dot_general x4, matrix products, normed_part(): grad_two = dot('tf,df->td', hidden_grads[s], expand_weight)  39 us
    dot_general x4, matrix products, on_device(): grad_act = dot('td,fd->tf', grad_blocks[s], contract_weight)  37.2 us
    dot_general x4, matrix products, normed_part(): grad_one = dot('cte,cde->td', grads_rows, attend_weight)  35.9 us
    ppermute x2, waiting for transfers between devices, gather_blocks(): blocks[ring - s] = lax.ppermute(blocks[(ring - s + 1) % ring], 'mp', down)  35.5 us
  transfers between devices with their start and end apart: 57, of which 27 were waited for; matrix products, arithmetic and copies ran while one was open for 38% of the time, Pallas kernels for 3%

profile of v2, /device:TPU:0, one launch (start us, length us, event | category | flops | bytes accessed | tf_op | source)
XLA Modules:
  0.0 1002.1 jit_solution(3464543925516586596)
XLA Ops:
  60.6 35.5 %collective-permute-done.1 = bf16[512,2048]{1,0:T(8,128)(2,1)} collective-permute-done((bf16[512,2048]{1,0:T(8,128)(2,1)}, bf16[512,2048]{1,0:T(8,128)(2,1)}, u32[]{:S(2)}, u32[]{:S(2)}) %collective-permute-start.1) | collective-permute-done | bytes 2097184 | tf_op jit(solution)/shard_map/ppermute | solution.py:313
  135.5 10.9 %constant_dynamic-update-slice_fusion.18 = (bf16[2048,2048]{1,0:T(8,128)(2,1)}, bf16[512,2048]{1,0:T(8,128)(2,1)S(1)}, f32[512,2048]{1,0:T(8,128)}) fusion(bf16[2048,2048]{1,0:T(8,128)(2,1)} %copy-done.27, s32[]{:T(128)S(6)} %select_n.571, f32[2048]{0:T(1024)S(1)} %copy-done.97, bf16[2048,2048]{1,0:T(8,128)(2,1)} %param.26, ...), kind=kOutput, calls=%fused_computation.301 | convolution fusion | flops 4307550208 | bytes 18903044 | tf_op jit(solution)/shard_map/td,df->tf/dot_general | solution.py:358
  173.1 10.7 %constant_dynamic-update-slice_fusion.17 = (bf16[2048,2048]{1,0:T(8,128)(2,1)}, bf16[512,2048]{1,0:T(8,128)(2,1)S(1)}, f32[512,2048]{1,0:T(8,128)}) fusion(bf16[2048,2048]{1,0:T(8,128)(2,1)} %get-tuple-element.67, s32[]{:T(128)S(6)} %select_n.573, f32[2048]{0:T(1024)S(1)} %copy-done.97, bf16[2048,2048]{1,0:T(8,128)(2,1)} %param.26, ...), kind=kOutput, calls=%fused_computation.300 | convolution fusion | flops 4307550208 | bytes 18903044 | tf_op jit(solution)/shard_map/td,df->tf/dot_general | solution.py:358
  205.4 29.6 %collective-permute-done.2 = bf16[512,2048]{1,0:T(8,128)(2,1)S(1)} collective-permute-done((bf16[512,2048]{1,0:T(8,128)(2,1)}, bf16[512,2048]{1,0:T(8,128)(2,1)S(1)}, u32[]{:S(2)}, u32[]{:S(2)}) %collective-permute-start.2) | collective-permute-done | bytes 2097184 | tf_op jit(solution)/shard_map/ppermute | solution.py:311
  244.4 27.4 %attend_forward.1 = (bf16[2048,512]{1,0:T(8,128)(2,1)S(1)}, bf16[2048,512]{1,0:T(8,128)(2,1)}, bf16[2048,512]{1,0:T(8,128)(2,1)}, bf16[2048,512]{1,0:T(8,128)(2,1)}, f32[2,2048,1]{2,1,0:T(8,128)}) custom-call(s32[1]{0:T(128)} %copy.63.lengths, f32[3,2048,512]{2,1,0:T(8,128)} %copy-done.2, f32[3,2048,512]{2,1,0:T(8,128)} %copy-done.2, ...), custom_call_target="tpu_custom_call" | custom-call | tf_op jit(solution)/shard_map/attend_forward/pallas_call | solution.py:180
  358.6 23.8 %convolution_convert_fusion.1 = bf16[2048,2048]{1,0:T(8,128)(2,1)} fusion(bf16[2048,2048]{1,0:T(8,128)(2,1)} %get-tuple-element.63, bf16[2048,2048]{1,0:T(8,128)(2,1)} %constant_dynamic-update-slice_fusion.12), kind=kOutput, calls=%fused_computation.9 | convolution fusion | flops 17184063488 | bytes 25165824 | tf_op jit(solution)/shard_map/tf,td->fd/dot_general | solution.py:376
  391.6 21.2 %convolution_convert_fusion = bf16[2048,2048]{1,0:T(8,128)(2,1)} fusion(bf16[2048,2048]{1,0:T(8,128)(2,1)} %get-tuple-element.87, bf16[2048,2048]{1,0:T(8,128)(2,1)S(1)} %get-tuple-element.150), kind=kOutput, calls=%fused_computation.8 | convolution fusion | flops 17184063488 | bytes 25165824 | tf_op jit(solution)/shard_map/td,tf->df/dot_general | solution.py:377
  414.9 33.2 %attend_backward.1 = bf16[3,2048,512]{2,1,0:T(8,128)(2,1)} custom-call(s32[1]{0:T(128)} %copy.63.lengths, bf16[2048,512]{1,0:T(8,128)(2,1)S(1)} %get-tuple-element.27.q_in, bf16[2048,512]{1,0:T(8,128)(2,1)} %get-tuple-element.28.k_in, bf16[2048,512]{1,0:T(8,128)(2,1)} %get-tuple-element.29.v_in, bf16[2048,512]{1,0:T(8,128)(2,1)} %fusion.119.grad_in, ...), custom_call_target="tpu_custom_call" | custom-call | tf_op jit(solution)/shard_map/attend_backward/pallas_call | solution.py:210
  499.3 15.8 %convert_bitcast_fusion = bf16[3,2048,512]{1,2,0:T(8,128)(2,1)} fusion(bf16[3,2048,512]{2,1,0:T(8,128)(2,1)S(1)} %copy-done.6, bf16[2048,2048]{1,0:T(8,128)(2,1)S(1)} %bitcast.163), kind=kOutput, calls=%fused_computation.12 | convolution fusion | flops 12888047616 | bytes 20971520 | tf_op jit(solution)/shard_map/td,cte->cde/dot_general | solution.py:396
  532.7 11.4 %fusion.44 = (f32[2048]{0:T(1024)}, f32[2048]{0:T(1024)}, f32[2048]{0:T(1024)}, f32[2048]{0:T(1024)}, bf16[512,2048]{1,0:T(8,128)(2,1)}) fusion(bf16[512,2048]{1,0:T(8,128)(2,1)S(1)} %copy-done.9, f32[512]{0:T(512)S(1)} %copy-done.85, f32[512]{0:T(512)S(1)} %copy-done.79, f32[512,2048]{1,0:T(8,128)} %fusion.167, f32[2048]{0:T(1024)S(1)} %copy-done.57, ...), kind=kOutput, calls=%fused_computation.68 | convolution fusion | flops 3234848768 | bytes 16306180 | tf_op jit(solution)/shard_map/cte,cde->td/dot_general | solution.py:405
  610.3 33.7 %collective-permute-done.5 = bf16[512,2048]{1,0:T(8,128)(2,1)} collective-permute-done((bf16[512,2048]{1,0:T(8,128)(2,1)}, bf16[512,2048]{1,0:T(8,128)(2,1)}, u32[]{:S(2)}, u32[]{:S(2)}) %collective-permute-start.5) | collective-permute-done | bytes 2097184 | tf_op jit(solution)/shard_map/ppermute | solution.py:331
  651.0 13.4 %collective-permute-done.18 = bf16[768,512]{1,0:T(8,128)(2,1)} collective-permute-done((bf16[768,512]{1,0:T(8,128)(2,1)}, bf16[768,512]{1,0:T(8,128)(2,1)}, u32[]{:S(2)}, u32[]{:S(2)}) %collective-permute-start.18) | collective-permute-done | bytes 786464 | tf_op jit(solution)/shard_map/ppermute | solution.py:248
  668.2 20.8 %collective-permute-done.10 = bf16[512,2048]{1,0:T(8,128)(2,1)S(1)} collective-permute-done((bf16[512,2048]{1,0:T(8,128)(2,1)S(1)}, bf16[512,2048]{1,0:T(8,128)(2,1)S(1)}, u32[]{:S(2)}, u32[]{:S(2)}) %collective-permute-start.10) | collective-permute-done | bytes 2097184 | tf_op jit(solution)/shard_map/ppermute | solution.py:331
  720.8 12.8 %collective-permute-done.14 = f32[13824]{0:T(1024)S(1)} collective-permute-done((f32[13824]{0:T(1024)S(1)}, f32[13824]{0:T(1024)S(1)}, u32[]{:S(2)}, u32[]{:S(2)}) %collective-permute-start.14) | collective-permute-done | bytes 55328 | tf_op jit(solution)/shard_map/ppermute | solution.py:237
  735.9 30.8 %collective-permute-done.20 = bf16[384,512]{1,0:T(8,128)(2,1)S(1)} collective-permute-done((bf16[384,512]{1,0:T(8,128)(2,1)S(1)}, bf16[384,512]{1,0:T(8,128)(2,1)S(1)}, u32[]{:S(2)}, u32[]{:S(2)}) %collective-permute-start.20) | collective-permute-done | bytes 393248 | tf_op jit(solution)/shard_map/ppermute | solution.py:248
  771.1 21.7 %collective-permute-done.48 = bf16[256,2048]{1,0:T(8,128)(2,1)S(1)} collective-permute-done((bf16[256,2048]{1,0:T(8,128)(2,1)S(1)}, bf16[256,2048]{1,0:T(8,128)(2,1)S(1)}, u32[]{:S(2)}, u32[]{:S(2)}) %collective-permute-start.48) | collective-permute-done | bytes 1048608 | tf_op jit(solution)/shard_map/ppermute | solution.py:248
  794.7 18.3 %collective-permute-done.38 = bf16[256,2048]{1,0:T(8,128)(2,1)S(1)} collective-permute-done((bf16[256,2048]{1,0:T(8,128)(2,1)S(1)}, bf16[256,2048]{1,0:T(8,128)(2,1)S(1)}, u32[]{:S(2)}, u32[]{:S(2)}) %collective-permute-start.38) | collective-permute-done | bytes 1048608 | tf_op jit(solution)/shard_map/ppermute | solution.py:248
  816.1 17.3 %collective-permute-done.21 = bf16[768,512]{1,0:T(8,128)(2,1)S(1)} collective-permute-done((bf16[768,512]{1,0:T(8,128)(2,1)S(1)}, bf16[768,512]{1,0:T(8,128)(2,1)S(1)}, u32[]{:S(2)}, u32[]{:S(2)}) %collective-permute-start.21) | collective-permute-done | bytes 786464 | tf_op jit(solution)/shard_map/ppermute | solution.py:248
  879.5 12.4 %collective-permute-done.40 = bf16[128,2048]{1,0:T(8,128)(2,1)S(1)} collective-permute-done((bf16[128,2048]{1,0:T(8,128)(2,1)S(1)}, bf16[128,2048]{1,0:T(8,128)(2,1)S(1)}, u32[]{:S(2)}, u32[]{:S(2)}) %collective-permute-start.40) | collective-permute-done | bytes 524320 | tf_op jit(solution)/shard_map/ppermute | solution.py:248
  893.7 18.0 %collective-permute-done.55 = bf16[256,2048]{1,0:T(8,128)(2,1)S(1)} collective-permute-done((bf16[256,2048]{1,0:T(8,128)(2,1)S(1)}, bf16[256,2048]{1,0:T(8,128)(2,1)S(1)}, u32[]{:S(2)}, u32[]{:S(2)}) %collective-permute-start.55) | collective-permute-done | bytes 1048608 | tf_op jit(solution)/shard_map/ppermute | solution.py:248
  915.9 16.8 %collective-permute-done.45 = bf16[256,2048]{1,0:T(8,128)(2,1)S(1)} collective-permute-done((bf16[256,2048]{1,0:T(8,128)(2,1)S(1)}, bf16[256,2048]{1,0:T(8,128)(2,1)S(1)}, u32[]{:S(2)}, u32[]{:S(2)}) %collective-permute-start.45) | collective-permute-done | bytes 1048608 | tf_op jit(solution)/shard_map/ppermute | solution.py:248
  966.4 11.2 %broadcast_select_fusion.1 = (bf16[1024,2048]{1,0:T(8,128)(2,1)}, bf16[1024,2048]{1,0:T(8,128)(2,1)}, bf16[1024,2048]{1,0:T(8,128)(2,1)}, bf16[1024,2048]{1,0:T(8,128)(2,1)}) fusion(bf16[1024,2048]{1,0:T(8,128)(2,1)} %collective-permute-done.56, pred[]{:T(512)S(6)} %eq.103, bf16[256,2048]{1,0:T(8,128)(2,1)S(1)} %copy-done.14, ...), kind=kLoop, calls=%fused_computation.145 | loop fusion | flops 41943040 | bytes 33554432 | tf_op jit(solution)/shard_map/jit(_where)/select_n | solution.py:261
  977.6 11.8 %maximum_convert_fusion = f32[2048,2048]{1,0:T(8,128)} fusion(bf16[1024,2048]{1,0:T(8,128)(2,1)} %get-tuple-element.154, bf16[1024,2048]{1,0:T(8,128)(2,1)} %get-tuple-element.155), kind=kLoop, calls=%fused_computation.2 | loop fusion | flops 16777216 | bytes 25165824 | tf_op jit(solution)/shard_map/concatenate | solution.py:273
  989.5 11.8 %maximum_convert_fusion.1 = f32[2048,2048]{1,0:T(8,128)} fusion(bf16[1024,2048]{1,0:T(8,128)(2,1)} %get-tuple-element.72, bf16[1024,2048]{1,0:T(8,128)(2,1)} %get-tuple-element.71), kind=kLoop, calls=%fused_computation.3 | loop fusion | flops 16777216 | bytes 25165824 | tf_op jit(solution)/shard_map/concatenate | solution.py:273
  (521 shorter events, 527.8 us)
Async XLA Ops:
  0.7 60.0 %collective-permute-start = (bf16[512,2048]{1,0:T(8,128)(2,1)}, bf16[512,2048]{1,0:T(8,128)(2,1)}, u32[]{:S(2)}, u32[]{:S(2)}) collective-permute-start(bf16[512,2048]{1,0:T(8,128)(2,1)} %param.15), channel_id=1, source_target_pairs={{0,1},{1,2},{2,3},{3,0},{4,5},{5,6},{6,7},{7,4},{8,9},{9,10},{10,1... | collective-permute-start | bytes 6291464 | tf_op jit(solution)/shard_map/ppermute | solution.py:311
  3.8 92.3 %collective-permute-start.1 = (bf16[512,2048]{1,0:T(8,128)(2,1)}, bf16[512,2048]{1,0:T(8,128)(2,1)}, u32[]{:S(2)}, u32[]{:S(2)}) collective-permute-start(bf16[512,2048]{1,0:T(8,128)(2,1)} %param.15), channel_id=1, source_target_pairs={{0,3},{1,0},{2,1},{3,2},{4,7},{5,4},{6,5},{7,6},{8,11},{9,8},{10,9... | collective-permute-start | bytes 6291464 | tf_op jit(solution)/shard_map/ppermute | solution.py:313
  96.1 183.4 %collective-permute-start.3 = (bf16[512,2048]{1,0:T(8,128)(2,1)}, bf16[512,2048]{1,0:T(8,128)(2,1)}, u32[]{:S(2)}, u32[]{:S(2)}) collective-permute-start(bf16[512,2048]{1,0:T(8,128)(2,1)} %get-tuple-element.24), channel_id=1, source_target_pairs={{0,1},{1,2},{2,3},{3,0},{4,5},{5,6},{6,7},{7,4},{8,9},{9,10},{10,1... | collective-permute-start | bytes 6291464 | tf_op jit(solution)/shard_map/ppermute | solution.py:311
  97.2 211.2 %collective-permute-start.8 = (bf16[512,2048]{1,0:T(8,128)(2,1)}, bf16[512,2048]{1,0:T(8,128)(2,1)}, u32[]{:S(2)}, u32[]{:S(2)}) collective-permute-start(bf16[512,2048]{1,0:T(8,128)(2,1)} %get-tuple-element.24), channel_id=1, source_target_pairs={{0,3},{1,0},{2,1},{3,2},{4,7},{5,4},{6,5},{7,6},{8,11},{9,8},{10,9... | collective-permute-start | bytes 6291464 | tf_op jit(solution)/shard_map/ppermute | solution.py:313
  161.1 74.0 %collective-permute-start.2 = (bf16[512,2048]{1,0:T(8,128)(2,1)}, bf16[512,2048]{1,0:T(8,128)(2,1)S(1)}, u32[]{:S(2)}, u32[]{:S(2)}) collective-permute-start(bf16[512,2048]{1,0:T(8,128)(2,1)} %collective-permute-done), channel_id=1, source_target_pairs={{0,1},{1,2},{2,3},{3,0},{4,5},{5,6},{6,7},{7,4},{8,9},{9,10},{10,1... | collective-permute-start | bytes 6291464 | tf_op jit(solution)/shard_map/ppermute | solution.py:311
  279.5 77.4 %collective-permute-start.4 = (bf16[512,2048]{1,0:T(8,128)(2,1)}, bf16[512,2048]{1,0:T(8,128)(2,1)S(1)}, u32[]{:S(2)}, u32[]{:S(2)}) collective-permute-start(bf16[512,2048]{1,0:T(8,128)(2,1)} %collective-permute-done.3), channel_id=1, source_target_pairs={{0,1},{1,2},{2,3},{3,0},{4,5},{5,6},{6,7},{7,4},{8,9},{9,10},{10,1... | collective-permute-start | bytes 6291464 | tf_op jit(solution)/shard_map/ppermute | solution.py:311
  485.0 181.6 %collective-permute-start.11 = (bf16[512,2048]{1,0:T(8,128)(2,1)}, bf16[512,2048]{1,0:T(8,128)(2,1)}, u32[]{:S(2)}, u32[]{:S(2)}) collective-permute-start(bf16[512,2048]{1,0:T(8,128)(2,1)} %get-tuple-element.75), channel_id=1, source_target_pairs={{0,3},{1,0},{2,1},{3,2},{4,7},{5,4},{6,5},{7,6},{8,11},{9,8},{10,9... | collective-permute-start | bytes 6291464 | tf_op jit(solution)/shard_map/ppermute | solution.py:331
  548.5 50.6 %collective-permute-start.9 = (bf16[512,2048]{1,0:T(8,128)(2,1)}, bf16[512,2048]{1,0:T(8,128)(2,1)}, u32[]{:S(2)}, u32[]{:S(2)}) collective-permute-start(bf16[512,2048]{1,0:T(8,128)(2,1)} %get-tuple-element.77), channel_id=1, source_target_pairs={{0,1},{1,2},{2,3},{3,0},{4,5},{5,6},{6,7},{7,4},{8,9},{9,10},{10,1... | collective-permute-start | bytes 6291464 | tf_op jit(solution)/shard_map/ppermute | solution.py:331
  548.5 95.6 %collective-permute-start.5 = (bf16[512,2048]{1,0:T(8,128)(2,1)}, bf16[512,2048]{1,0:T(8,128)(2,1)}, u32[]{:S(2)}, u32[]{:S(2)}) collective-permute-start(bf16[512,2048]{1,0:T(8,128)(2,1)} %add_convert_fusion.5), channel_id=1, source_target_pairs={{0,1},{1,2},{2,3},{3,0},{4,5},{5,6},{6,7},{7,4},{8,9},{9,10},{10,1... | collective-permute-start | bytes 6291464 | tf_op jit(solution)/shard_map/ppermute | solution.py:331
  549.1 57.2 %collective-permute-start.17 = (bf16[3072,512]{1,0:T(8,128)(2,1)}, bf16[3072,512]{1,0:T(8,128)(2,1)S(1)}, u32[]{:S(2)}, u32[]{:S(2)}) collective-permute-start(bf16[3072,512]{1,0:T(8,128)(2,1)} %constant_dynamic-slice_fusion.19), channel_id=1, source_target_pairs={{0,4},{4,0},{8,12},{12,8},{16,20},{20,16},{24,28},{28,24},{1,5},{5... | collective-permute-start | bytes 9437192 | tf_op jit(solution)/shard_map/ppermute | solution.py:248
  588.7 109.2 %collective-permute-start.47 = (bf16[1024,2048]{1,0:T(8,128)(2,1)}, bf16[1024,2048]{1,0:T(8,128)(2,1)}, u32[]{:S(2)}, u32[]{:S(2)}) collective-permute-start(bf16[1024,2048]{1,0:T(8,128)(2,1)} %constant_dynamic-slice_fusion.4), channel_id=1, source_target_pairs={{0,4},{4,0},{8,12},{12,8},{16,20},{20,16},{24,28},{28,24},{1,5},{5... | collective-permute-start | bytes 12582920 | tf_op jit(solution)/shard_map/ppermute | solution.py:248
  606.4 82.6 %collective-permute-start.10 = (bf16[512,2048]{1,0:T(8,128)(2,1)S(1)}, bf16[512,2048]{1,0:T(8,128)(2,1)S(1)}, u32[]{:S(2)}, u32[]{:S(2)}) collective-permute-start(bf16[512,2048]{1,0:T(8,128)(2,1)S(1)} %get-tuple-element.76), channel_id=1, source_target_pairs={{0,1},{1,2},{2,3},{3,0},{4,5},{5,6},{6,7},{7,4},{8,9},{9,10},{10,1... | collective-permute-start | bytes 6291464 | tf_op jit(solution)/shard_map/ppermute | solution.py:331
  607.6 36.5 %collective-permute-start.22 = (bf16[768,512]{1,0:T(8,128)(2,1)S(1)}, bf16[768,512]{1,0:T(8,128)(2,1)S(1)}, u32[]{:S(2)}, u32[]{:S(2)}) collective-permute-start(bf16[768,512]{1,0:T(8,128)(2,1)S(1)} %constant_dynamic-slice_fusion.16), channel_id=1, source_target_pairs={{0,16},{4,20},{8,24},{12,28},{16,0},{20,4},{24,8},{28,12},{1,17},{... | collective-permute-start | bytes 2359304 | tf_op jit(solution)/shard_map/ppermute | solution.py:248
  644.1 62.2 %collective-permute-start.37 = (bf16[1024,2048]{1,0:T(8,128)(2,1)}, bf16[1024,2048]{1,0:T(8,128)(2,1)}, u32[]{:S(2)}, u32[]{:S(2)}) collective-permute-start(bf16[1024,2048]{1,0:T(8,128)(2,1)} %constant_dynamic-slice_fusion.9), channel_id=1, source_target_pairs={{0,4},{4,0},{8,12},{12,8},{16,20},{20,16},{24,28},{28,24},{1,5},{5... | collective-permute-start | bytes 12582920 | tf_op jit(solution)/shard_map/ppermute | solution.py:248
  664.4 278.2 %collective-permute-start.7 = (bf16[512,2048]{1,0:T(8,128)(2,1)}, bf16[512,2048]{1,0:T(8,128)(2,1)}, u32[]{:S(2)}, u32[]{:S(2)}) collective-permute-start(bf16[512,2048]{1,0:T(8,128)(2,1)} %add_convert_fusion.3), channel_id=1, source_target_pairs={{0,3},{1,0},{2,1},{3,2},{4,7},{5,4},{6,5},{7,6},{8,11},{9,8},{10,9... | collective-permute-start | bytes 6291464 | tf_op jit(solution)/shard_map/ppermute | solution.py:331
  666.6 49.8 %collective-permute-start.23 = (bf16[384,512]{1,0:T(8,128)(2,1)}, bf16[384,512]{1,0:T(8,128)(2,1)}, u32[]{:S(2)}, u32[]{:S(2)}) collective-permute-start(bf16[384,512]{1,0:T(8,128)(2,1)} %constant_dynamic-slice_fusion.15), channel_id=1, source_target_pairs={{0,8},{4,12},{8,0},{12,4},{16,24},{20,28},{24,16},{28,20},{1,9},{5... | collective-permute-start | bytes 1179656 | tf_op jit(solution)/shard_map/ppermute | solution.py:248
  706.8 61.6 %collective-permute-start.52 = (bf16[256,2048]{1,0:T(8,128)(2,1)}, bf16[256,2048]{1,0:T(8,128)(2,1)}, u32[]{:S(2)}, u32[]{:S(2)}) collective-permute-start(bf16[256,2048]{1,0:T(8,128)(2,1)} %constant_dynamic-slice_fusion.1), channel_id=1, source_target_pairs={{0,16},{4,20},{8,24},{12,28},{16,0},{20,4},{24,8},{28,12},{1,17},{... | collective-permute-start | bytes 3145736 | tf_op jit(solution)/shard_map/ppermute | solution.py:248
  719.1 219.6 %collective-permute-start.36 = (bf16[256,2048]{1,0:T(8,128)(2,1)}, bf16[256,2048]{1,0:T(8,128)(2,1)S(1)}, u32[]{:S(2)}, u32[]{:S(2)}) collective-permute-start(bf16[256,2048]{1,0:T(8,128)(2,1)} %pad_maximum_fusion.4), channel_id=1, source_target_pairs={{0,4},{4,0},{8,12},{12,8},{16,20},{20,16},{24,28},{28,24},{1,5},{5... | collective-permute-start | bytes 3145736 | tf_op jit(solution)/shard_map/ppermute | solution.py:248
  733.6 36.9 %collective-permute-start.42 = (bf16[256,2048]{1,0:T(8,128)(2,1)S(1)}, bf16[256,2048]{1,0:T(8,128)(2,1)S(1)}, u32[]{:S(2)}, u32[]{:S(2)}) collective-permute-start(bf16[256,2048]{1,0:T(8,128)(2,1)S(1)} %constant_dynamic-slice_fusion.6), channel_id=1, source_target_pairs={{0,16},{4,20},{8,24},{12,28},{16,0},{20,4},{24,8},{28,12},{1,17},{... | collective-permute-start | bytes 3145736 | tf_op jit(solution)/shard_map/ppermute | solution.py:248
  735.2 31.6 %collective-permute-start.20 = (bf16[384,512]{1,0:T(8,128)(2,1)S(1)}, bf16[384,512]{1,0:T(8,128)(2,1)S(1)}, u32[]{:S(2)}, u32[]{:S(2)}) collective-permute-start(bf16[384,512]{1,0:T(8,128)(2,1)S(1)} %add_convert_fusion.18), channel_id=1, source_target_pairs={{0,16},{4,20},{8,24},{12,28},{16,0},{20,4},{24,8},{28,12},{1,17},{... | collective-permute-start | bytes 1179656 | tf_op jit(solution)/shard_map/ppermute | solution.py:248
  768.3 44.7 %collective-permute-start.38 = (bf16[256,2048]{1,0:T(8,128)(2,1)S(1)}, bf16[256,2048]{1,0:T(8,128)(2,1)S(1)}, u32[]{:S(2)}, u32[]{:S(2)}) collective-permute-start(bf16[256,2048]{1,0:T(8,128)(2,1)S(1)} %constant_dynamic-slice_fusion.8), channel_id=1, source_target_pairs={{0,8},{4,12},{8,0},{12,4},{16,24},{20,28},{24,16},{28,20},{1,9},{5... | collective-permute-start | bytes 3145736 | tf_op jit(solution)/shard_map/ppermute | solution.py:248
  770.6 172.2 %collective-permute-start.6 = (bf16[512,2048]{1,0:T(8,128)(2,1)S(1)}, bf16[512,2048]{1,0:T(8,128)(2,1)S(1)}, u32[]{:S(2)}, u32[]{:S(2)}) collective-permute-start(bf16[512,2048]{1,0:T(8,128)(2,1)S(1)} %copy-done.55), channel_id=1, source_target_pairs={{0,1},{1,2},{2,3},{3,0},{4,5},{5,6},{6,7},{7,4},{8,9},{9,10},{10,1... | collective-permute-start | bytes 6291464 | tf_op jit(solution)/shard_map/ppermute | solution.py:331
  815.1 29.5 %collective-permute-start.53 = (bf16[128,2048]{1,0:T(8,128)(2,1)S(1)}, bf16[128,2048]{1,0:T(8,128)(2,1)S(1)}, u32[]{:S(2)}, u32[]{:S(2)}) collective-permute-start(bf16[128,2048]{1,0:T(8,128)(2,1)S(1)} %constant_dynamic-slice_fusion), channel_id=1, source_target_pairs={{0,8},{4,12},{8,0},{12,4},{16,24},{20,28},{24,16},{28,20},{1,9},{5... | collective-permute-start | bytes 1572872 | tf_op jit(solution)/shard_map/ppermute | solution.py:248
  878.8 33.0 %collective-permute-start.55 = (bf16[256,2048]{1,0:T(8,128)(2,1)S(1)}, bf16[256,2048]{1,0:T(8,128)(2,1)S(1)}, u32[]{:S(2)}, u32[]{:S(2)}) collective-permute-start(bf16[256,2048]{1,0:T(8,128)(2,1)S(1)} %pad_maximum_fusion.8), channel_id=1, source_target_pairs={{0,16},{4,20},{8,24},{12,28},{16,0},{20,4},{24,8},{28,12},{1,17},{... | collective-permute-start | bytes 3145736 | tf_op jit(solution)/shard_map/ppermute | solution.py:248
  (152 other events, 2997.2 us)
